TPU v7x, 32 devices: a whole 2x2x4 slice. The times are simulated.
32 devices in a mesh: groups: 2 (over x), blk: 16 (over z, y, core).
Axes of the slice: x: 2, y: 2, z: 4, core: 2. Of those that a mesh axis runs over, the one named last changes fastest.
Arguments:
- embeddings: bfloat16 [16384, 768], P(('groups', 'blk')), parts along dimension 0
- doc_order: int32 [16384], P(('groups', 'blk')), parts along dimension 0, may hold values from 0 to 8191, each once
- neighbours: int32 [32, 4], P('groups'), parts along dimension 0, may hold values from 0 to 15, as said below
Outputs:
- earlier_max: float32 [16384], P(('groups', 'blk')), parts along dimension 0
- later_max: bfloat16 [16384], P(('groups', 'blk')), parts along dimension 0
There are 2 independent parts, one for each index of `groups`. A program takes and returns all parts, laid end to end along the dimension named above; each array names one. Nothing has to cross between parts.
Inputs may be any that keep to these rules, and one draw needn't show every extreme that they name: Every entry of neighbours[b] is a block at distance at most 2 from b along the loop of 16 blocks, (b + k) mod 16 with -2 <= k <= 2; block 0 lists both blocks at distance 2; a block may list an entry several times or list itself.
All inputs are finite; a program needn't handle non-finite values.
Results may differ from a plain program's by a relative error of at most 0.0028.
Values may be sent and summed in bfloat16 or wider, within the bound.
No kernel may reach another device: no remote copies, remote signals or barrier semaphores. Data moves between devices by JAX's collectives and lax.ppermute only.
A program may use at most 64 MiB of HBM per device.

v0:
```python
import jax
import jax.numpy as jnp
from jax import lax
from jax.sharding import PartitionSpec as P

REACH = 2


def from_behind(x, axis, by):
    peers = lax.axis_size(axis)
    return lax.ppermute(x, axis, [(i, (i + by) % peers) for i in range(peers)])


def normalize(embeddings):
    values = embeddings.astype(jnp.float32)
    inverse = lax.rsqrt(jnp.sum(values * values, axis=-1, keepdims=True) + 1e-06)
    return (values * inverse).astype(jnp.bfloat16)


def pair_scores(unit_rows, order_rows, unit_cols, order_cols, listed):
    scores = lax.dot_general(
        unit_rows, unit_cols, (((1,), (1,)), ((), ())), preferred_element_type=jnp.float32
    )
    valid = jnp.logical_and(order_cols[None, :] < order_rows[:, None], listed)
    return jnp.where(valid, scores, jnp.float32(-1.0))


def local(embeddings, doc_order, neighbours):
    rows_now = embeddings.shape[0]
    blocks = lax.axis_size("blk")
    here = lax.axis_index("blk")
    unit_rows = normalize(embeddings)
    my_list = lax.dynamic_index_in_dim(neighbours, here, 0, keepdims=False)

    def visit(row_best, unit_cols, order_cols, block_id):
        listed = jnp.any(my_list == block_id)
        masked = pair_scores(unit_rows, doc_order, unit_cols, order_cols, listed)
        return (
            jnp.maximum(row_best, jnp.max(masked, axis=1)),
            jnp.max(masked, axis=0).astype(jnp.bfloat16),
        )

    own_masked = pair_scores(unit_rows, doc_order, unit_rows, doc_order, True)
    row_best = jnp.max(own_masked, axis=1)
    later = jnp.max(own_masked, axis=0).astype(jnp.bfloat16)
    empty_col = jnp.full((rows_now,), -1.0, jnp.bfloat16)
    up_units, up_order, up_travel = (unit_rows, doc_order, empty_col)
    for step in range(1, REACH + 1):
        up_units, up_order, up_travel = from_behind((up_units, up_order, up_travel), "blk", 1)
        row_best, col_part = visit(row_best, up_units, up_order, (here - step) % blocks)
        up_travel = jnp.maximum(up_travel, col_part)
    down_units, down_order, down_travel = (unit_rows, doc_order, empty_col)
    for step in range(1, REACH + 1):
        down_units, down_order, down_travel = from_behind(
            (down_units, down_order, down_travel), "blk", -1
        )
        row_best, col_part = visit(row_best, down_units, down_order, (here + step) % blocks)
        down_travel = jnp.maximum(down_travel, col_part)
    later = jnp.maximum(later, from_behind(up_travel, "blk", -REACH))
    later = jnp.maximum(later, from_behind(down_travel, "blk", REACH))
    return (row_best, later)


def solution(mesh):
    placed = (P(("groups", "blk"), None), P(("groups", "blk")), P("groups", None))
    return jax.shard_map(
        local,
        mesh=mesh,
        in_specs=placed,
        out_specs=(P(("groups", "blk")), P(("groups", "blk"))),
        check_vma=False,
    )
```

profile of v0, /device:TPU:0, one launch (start us, length us, event | category | flops | bytes accessed | tf_op | source)
XLA Modules:
  0.0 63.2 jit_solution(10614746640065709251)
XLA Ops:
  0.7 1.4 %fusion = f32[512]{0:T(512)S(1)} fusion(bf16[512,768]{1,0:T(8,128)(2,1)} %param.3), kind=kLoop, calls=%fused_computation.2 | loop fusion | flops 1179136 | bytes 788480 | tf_op jit(solution)/shard_map/reduce_sum | solution.py:16
  2.3 5.5 %collective-permute-start.5 = (bf16[512,768]{1,0:T(8,128)(2,1)S(1)}, bf16[512,768]{1,0:T(8,128)(2,1)S(1)}, u32[]{:S(2)}, u32[]{:S(2)}) collective-permute-start(bf16[512,768]{1,0:T(8,128)(2,1)S(1)} %fusion.1), channel_id=1, source_target_pairs={{0,15},{1,0},{2,1},{3,2},{4,3},{5,4},{6,5},{7,6},{8,7},{9,8},{10,9... | collective-permute-start | bytes 2359304 | tf_op jit(solution)/shard_map/ppermute | solution.py:11
  7.8 9.5 %collective-permute-done.5 = bf16[512,768]{1,0:T(8,128)(2,1)S(1)} collective-permute-done((bf16[512,768]{1,0:T(8,128)(2,1)S(1)}, bf16[512,768]{1,0:T(8,128)(2,1)S(1)}, u32[]{:S(2)}, u32[]{:S(2)}) %collective-permute-start.5) | collective-permute-done | bytes 786464 | tf_op jit(solution)/shard_map/ppermute | solution.py:11
  17.3 4.7 %collective-permute-start.7 = (bf16[512,768]{1,0:T(8,128)(2,1)S(1)}, bf16[512,768]{1,0:T(8,128)(2,1)S(1)}, u32[]{:S(2)}, u32[]{:S(2)}) collective-permute-start(bf16[512,768]{1,0:T(8,128)(2,1)S(1)} %collective-permute-done.5), channel_id=1, source_target_pairs={{0,15},{1,0},{2,1},{3,2},{4,3},{5,4},{6,5},{7,6},{8,7},{9,8},{10,9... | collective-permute-start | bytes 2359304 | tf_op jit(solution)/shard_map/ppermute | solution.py:11
  22.1 1.5 %collective-permute-start = (s32[512]{0:T(512)S(1)}, s32[512]{0:T(512)S(1)}, u32[]{:S(2)}, u32[]{:S(2)}) collective-permute-start(s32[512]{0:T(512)S(1)} %copy-done.2), channel_id=1, source_target_pairs={{0,1},{1,2},{2,3},{3,4},{4,5},{5,6},{6,7},{7,8},{8,9},{9,10},{10,1... | collective-permute-start | bytes 6152 | tf_op jit(solution)/shard_map/ppermute | solution.py:11
  23.6 2.9 %collective-permute-start.4 = (s32[512]{0:T(512)S(1)}, s32[512]{0:T(512)S(1)}, u32[]{:S(2)}, u32[]{:S(2)}) collective-permute-start(s32[512]{0:T(512)S(1)} %copy-done.2), channel_id=1, source_target_pairs={{0,15},{1,0},{2,1},{3,2},{4,3},{5,4},{6,5},{7,6},{8,7},{9,8},{10,9... | collective-permute-start | bytes 6152 | tf_op jit(solution)/shard_map/ppermute | solution.py:11
  26.5 0.8 %compare_reduce_fusion.3 = (pred[]{:T(512)}, pred[]{:T(512)}, pred[]{:T(512)}, pred[]{:T(512)}) fusion(s32[]{:T(128)S(6)} %select_n.41, s32[16,4]{0,1:T(4,128)S(1)} %copy-done.1, s32[]{:T(128)S(6)} %select_n.40, s32[]{:T(128)S(6)} %select_n.43, s32[]{:T(128)S(6)} %select_n.45, s32[]{:T(128)S(6)} %select_n.47), kind=kLoop, calls=%fused_computation.22 | loop fusion | flops 28 | bytes 40 | tf_op jit(solution)/shard_map/reduce_or | solution.py:36
  27.3 4.0 %collective-permute-start.3 = (bf16[512,768]{1,0:T(8,128)(2,1)S(1)}, bf16[512,768]{1,0:T(8,128)(2,1)S(1)}, u32[]{:S(2)}, u32[]{:S(2)}) collective-permute-start(bf16[512,768]{1,0:T(8,128)(2,1)S(1)} %collective-permute-done.1), channel_id=1, source_target_pairs={{0,1},{1,2},{2,3},{3,4},{4,5},{5,6},{6,7},{7,8},{8,9},{9,10},{10,1... | collective-permute-start | bytes 2359304 | tf_op jit(solution)/shard_map/ppermute | solution.py:11
  31.4 0.6 fusion.12
  32.0 0.6 fusion.11
  32.6 0.5 collective-permute-start.11
  33.1 10.4 %collective-permute-start.2 = (s32[512]{0:T(512)S(1)}, s32[512]{0:T(512)S(1)}, u32[]{:S(2)}, u32[]{:S(2)}) collective-permute-start(s32[512]{0:T(512)S(1)} %collective-permute-done), channel_id=1, source_target_pairs={{0,1},{1,2},{2,3},{3,4},{4,5},{5,6},{6,7},{7,8},{8,9},{9,10},{10,1... | collective-permute-start | bytes 6152 | tf_op jit(solution)/shard_map/ppermute | solution.py:11
  43.5 0.6 fusion.13
  44.3 0.5 collective-permute-done.6
  44.8 3.8 %fusion.4 = (bf16[512]{0:T(512)(128)(2,1)S(1)}, f32[512]{0:T(512)S(1)}, f32[512]{0:T(512)S(1)}, bf16[512]{0:T(512)(128)(2,1)S(1)}, f32[512]{0:T(512)S(1)}, /*ind...) fusion(s32[512]{0:T(512)S(1)} %collective-permute-done.2, pred[]{:T(512)} %get-tuple-element.19, ...), kind=kOutput, calls=%fused_computation.11 | convolution fusion | flops 407891968 | bytes 4741124 | tf_op jit(solution)/shard_map/dot_general | solution.py:21
  48.6 1.7 %collective-permute-start.9 = (bf16[512]{0:T(512)(128)(2,1)S(1)}, bf16[512]{0:T(512)(128)(2,1)S(1)}, u32[]{:S(2)}, u32[]{:S(2)}) collective-permute-start(bf16[512]{0:T(512)(128)(2,1)S(1)} %max.53), channel_id=1, source_target_pairs={{0,1},{1,2},{2,3},{3,4},{4,5},{5,6},{6,7},{7,8},{8,9},{9,10},{10,1... | collective-permute-start | bytes 3080 | tf_op jit(solution)/shard_map/ppermute | solution.py:11
  50.4 2.8 %collective-permute-start.12 = (bf16[512]{0:T(512)(128)(2,1)S(1)}, bf16[512]{0:T(512)(128)(2,1)S(1)}, u32[]{:S(2)}, u32[]{:S(2)}) collective-permute-start(bf16[512]{0:T(512)(128)(2,1)S(1)} %max.51), channel_id=1, source_target_pairs={{0,15},{1,0},{2,1},{3,2},{4,3},{5,4},{6,5},{7,6},{8,7},{9,8},{10,9... | collective-permute-start | bytes 3080 | tf_op jit(solution)/shard_map/ppermute | solution.py:11
  53.1 0.7 %fusion.10 = (bf16[512]{0:T(512)(128)(2,1)S(1)}, f32[512]{0:T(512)S(1)}) fusion(bf16[512,768]{1,0:T(8,128)(2,1)S(1)} %fusion.1, s32[512]{0:T(512)S(1)} %copy-done.2), kind=kOutput, calls=%fused_computation.28 | convolution fusion | flops 403700736 | bytes 791552 | tf_op jit(solution)/shard_map/dot_general | solution.py:21
  53.8 0.5 collective-permute-done.9
  54.4 1.9 %collective-permute-start.10 = (bf16[512]{0:T(512)(128)(2,1)S(1)}, bf16[512]{0:T(512)(128)(2,1)S(1)}, u32[]{:S(2)}, u32[]{:S(2)}) collective-permute-start(bf16[512]{0:T(512)(128)(2,1)S(1)} %max.52), channel_id=1, source_target_pairs={{0,14},{1,15},{2,0},{3,1},{4,2},{5,3},{6,4},{7,5},{8,6},{9,7},{10,... | collective-permute-start | bytes 3080 | tf_op jit(solution)/shard_map/ppermute | solution.py:11
  56.4 0.6 maximum_maximum_fusion
  57.0 0.9 %collective-permute-done.10 = bf16[512]{0:T(512)(128)(2,1)S(1)} collective-permute-done((bf16[512]{0:T(512)(128)(2,1)S(1)}, bf16[512]{0:T(512)(128)(2,1)S(1)}, u32[]{:S(2)}, u32[]{:S(2)}) %collective-permute-start.10) | collective-permute-done | bytes 1056 | tf_op jit(solution)/shard_map/ppermute | solution.py:11
  57.9 4.7 %collective-permute-done.13 = bf16[512]{0:T(512)(128)(2,1)S(1)} collective-permute-done((bf16[512]{0:T(512)(128)(2,1)S(1)}, bf16[512]{0:T(512)(128)(2,1)S(1)}, u32[]{:S(2)}, u32[]{:S(2)}) %collective-permute-start.13) | collective-permute-done | bytes 1056 | tf_op jit(solution)/shard_map/ppermute | solution.py:11
  62.6 0.6 maximum_maximum_fusion.1
  (26 shorter events, 0.6 us)
Async XLA Ops:
  0.6 1.5 %copy-start = (bf16[512,768]{1,0:T(8,128)(2,1)S(1)}, bf16[512,768]{1,0:T(8,128)(2,1)}, u32[]{:S(2)}) copy-start(bf16[512,768]{1,0:T(8,128)(2,1)} %param.3) | copy-start | bytes 2359300
  0.6 21.4 %copy-start.2 = (s32[512]{0:T(512)S(1)}, s32[512]{0:T(512)}, u32[]{:S(2)}) copy-start(s32[512]{0:T(512)} %param.4) | copy-start | bytes 6148
  0.6 25.9 %copy-start.1 = (s32[16,4]{0,1:T(4,128)S(1)}, s32[16,4]{0,1:T(4,128)}, u32[]{:S(2)}) copy-start(s32[16,4]{0,1:T(4,128)} %param.5) | copy-start | bytes 772
  2.3 15.0 %collective-permute-start.5 = (bf16[512,768]{1,0:T(8,128)(2,1)S(1)}, bf16[512,768]{1,0:T(8,128)(2,1)S(1)}, u32[]{:S(2)}, u32[]{:S(2)}) collective-permute-start(bf16[512,768]{1,0:T(8,128)(2,1)S(1)} %fusion.1), channel_id=1, source_target_pairs={{0,15},{1,0},{2,1},{3,2},{4,3},{5,4},{6,5},{7,6},{8,7},{9,8},{10,9... | collective-permute-start | bytes 2359304 | tf_op jit(solution)/shard_map/ppermute | solution.py:11
  7.8 19.5 %collective-permute-start.1 = (bf16[512,768]{1,0:T(8,128)(2,1)S(1)}, bf16[512,768]{1,0:T(8,128)(2,1)S(1)}, u32[]{:S(2)}, u32[]{:S(2)}) collective-permute-start(bf16[512,768]{1,0:T(8,128)(2,1)S(1)} %fusion.1), channel_id=1, source_target_pairs={{0,1},{1,2},{2,3},{3,4},{4,5},{5,6},{6,7},{7,8},{8,9},{9,10},{10,1... | collective-permute-start | bytes 2359304 | tf_op jit(solution)/shard_map/ppermute | solution.py:11
  17.3 26.2 %collective-permute-start.7 = (bf16[512,768]{1,0:T(8,128)(2,1)S(1)}, bf16[512,768]{1,0:T(8,128)(2,1)S(1)}, u32[]{:S(2)}, u32[]{:S(2)}) collective-permute-start(bf16[512,768]{1,0:T(8,128)(2,1)S(1)} %collective-permute-done.5), channel_id=1, source_target_pairs={{0,15},{1,0},{2,1},{3,2},{4,3},{5,4},{6,5},{7,6},{8,7},{9,8},{10,9... | collective-permute-start | bytes 2359304 | tf_op jit(solution)/shard_map/ppermute | solution.py:11
  22.1 10.5 %collective-permute-start = (s32[512]{0:T(512)S(1)}, s32[512]{0:T(512)S(1)}, u32[]{:S(2)}, u32[]{:S(2)}) collective-permute-start(s32[512]{0:T(512)S(1)} %copy-done.2), channel_id=1, source_target_pairs={{0,1},{1,2},{2,3},{3,4},{4,5},{5,6},{6,7},{7,8},{8,9},{9,10},{10,1... | collective-permute-start | bytes 6152 | tf_op jit(solution)/shard_map/ppermute | solution.py:11
  23.6 9.5 %collective-permute-start.4 = (s32[512]{0:T(512)S(1)}, s32[512]{0:T(512)S(1)}, u32[]{:S(2)}, u32[]{:S(2)}) collective-permute-start(s32[512]{0:T(512)S(1)} %copy-done.2), channel_id=1, source_target_pairs={{0,15},{1,0},{2,1},{3,2},{4,3},{5,4},{6,5},{7,6},{8,7},{9,8},{10,9... | collective-permute-start | bytes 6152 | tf_op jit(solution)/shard_map/ppermute | solution.py:11
  26.5 22.1 %collective-permute-start.8 = (bf16[512]{0:T(512)(128)(2,1)S(1)}, bf16[512]{0:T(512)(128)(2,1)S(1)}, u32[]{:S(2)}, u32[]{:S(2)}) collective-permute-start(bf16[512]{0:T(512)(128)(2,1)S(1)} %broadcast_in_dim.11), channel_id=1, source_target_pairs={{0,1},{1,2},{2,3},{3,4},{4,5},{5,6},{6,7},{7,8},{8,9},{9,10},{10,1... | collective-permute-start | bytes 3080 | tf_op jit(solution)/shard_map/ppermute | solution.py:11
  27.3 17.5 %collective-permute-start.3 = (bf16[512,768]{1,0:T(8,128)(2,1)S(1)}, bf16[512,768]{1,0:T(8,128)(2,1)S(1)}, u32[]{:S(2)}, u32[]{:S(2)}) collective-permute-start(bf16[512,768]{1,0:T(8,128)(2,1)S(1)} %collective-permute-done.1), channel_id=1, source_target_pairs={{0,1},{1,2},{2,3},{3,4},{4,5},{5,6},{6,7},{7,8},{8,9},{9,10},{10,1... | collective-permute-start | bytes 2359304 | tf_op jit(solution)/shard_map/ppermute | solution.py:11
  32.6 17.8 %collective-permute-start.11 = (bf16[512]{0:T(512)(128)(2,1)S(1)}, bf16[512]{0:T(512)(128)(2,1)S(1)}, u32[]{:S(2)}, u32[]{:S(2)}) collective-permute-start(bf16[512]{0:T(512)(128)(2,1)S(1)} %broadcast_in_dim.11), channel_id=1, source_target_pairs={{0,15},{1,0},{2,1},{3,2},{4,3},{5,4},{6,5},{7,6},{8,7},{9,8},{10,9... | collective-permute-start | bytes 3080 | tf_op jit(solution)/shard_map/ppermute | solution.py:11
  33.1 11.3 %collective-permute-start.2 = (s32[512]{0:T(512)S(1)}, s32[512]{0:T(512)S(1)}, u32[]{:S(2)}, u32[]{:S(2)}) collective-permute-start(s32[512]{0:T(512)S(1)} %collective-permute-done), channel_id=1, source_target_pairs={{0,1},{1,2},{2,3},{3,4},{4,5},{5,6},{6,7},{7,8},{8,9},{9,10},{10,1... | collective-permute-start | bytes 6152 | tf_op jit(solution)/shard_map/ppermute | solution.py:11
  43.5 1.3 %collective-permute-start.6 = (s32[512]{0:T(512)S(1)}, s32[512]{0:T(512)S(1)}, u32[]{:S(2)}, u32[]{:S(2)}) collective-permute-start(s32[512]{0:T(512)S(1)} %collective-permute-done.4), channel_id=1, source_target_pairs={{0,15},{1,0},{2,1},{3,2},{4,3},{5,4},{6,5},{7,6},{8,7},{9,8},{10,9... | collective-permute-start | bytes 6152 | tf_op jit(solution)/shard_map/ppermute | solution.py:11
  48.6 5.7 %collective-permute-start.9 = (bf16[512]{0:T(512)(128)(2,1)S(1)}, bf16[512]{0:T(512)(128)(2,1)S(1)}, u32[]{:S(2)}, u32[]{:S(2)}) collective-permute-start(bf16[512]{0:T(512)(128)(2,1)S(1)} %max.53), channel_id=1, source_target_pairs={{0,1},{1,2},{2,3},{3,4},{4,5},{5,6},{6,7},{7,8},{8,9},{9,10},{10,1... | collective-permute-start | bytes 3080 | tf_op jit(solution)/shard_map/ppermute | solution.py:11
  50.4 5.9 %collective-permute-start.12 = (bf16[512]{0:T(512)(128)(2,1)S(1)}, bf16[512]{0:T(512)(128)(2,1)S(1)}, u32[]{:S(2)}, u32[]{:S(2)}) collective-permute-start(bf16[512]{0:T(512)(128)(2,1)S(1)} %max.51), channel_id=1, source_target_pairs={{0,15},{1,0},{2,1},{3,2},{4,3},{5,4},{6,5},{7,6},{8,7},{9,8},{10,9... | collective-permute-start | bytes 3080 | tf_op jit(solution)/shard_map/ppermute | solution.py:11
  54.4 3.6 %collective-permute-start.10 = (bf16[512]{0:T(512)(128)(2,1)S(1)}, bf16[512]{0:T(512)(128)(2,1)S(1)}, u32[]{:S(2)}, u32[]{:S(2)}) collective-permute-start(bf16[512]{0:T(512)(128)(2,1)S(1)} %max.52), channel_id=1, source_target_pairs={{0,14},{1,15},{2,0},{3,1},{4,2},{5,3},{6,4},{7,5},{8,6},{9,7},{10,... | collective-permute-start | bytes 3080 | tf_op jit(solution)/shard_map/ppermute | solution.py:11
  56.3 6.3 %collective-permute-start.13 = (bf16[512]{0:T(512)(128)(2,1)S(1)}, bf16[512]{0:T(512)(128)(2,1)S(1)}, u32[]{:S(2)}, u32[]{:S(2)}) collective-permute-start(bf16[512]{0:T(512)(128)(2,1)S(1)} %max.50), channel_id=1, source_target_pairs={{0,2},{1,3},{2,4},{3,5},{4,6},{5,7},{6,8},{7,9},{8,10},{9,11},{10,... | collective-permute-start | bytes 3080 | tf_op jit(solution)/shard_map/ppermute | solution.py:11
where the time goes:
time: 63.4 us; the launch traced here: 63.2 us
  starting transfers between devices  36.2 us (57%)
  waiting for transfers between devices  16.3 us (26%)
  matrix products  6.25 us (10%)
  other arithmetic  3.63 us (6%)
  between operations  0.73 us (1%)
    ppermute x14, starting transfers between devices, from_behind(): return lax.ppermute(x, axis, [(i, (i + by) % peers) for i in range(peers)])  36.2 us
    ppermute x14, waiting for transfers between devices, from_behind(): return lax.ppermute(x, axis, [(i, (i + by) % peers) for i in range(peers)])  16.3 us
    dot_general x5, matrix products, pair_scores(): lax.dot_general(unit_rows, unit_cols, (((1,), (1,)), ((), ())), preferred...  6.25 us
    reduce_sum x1, other arithmetic, normalize(): jnp.sum(values * values, axis=-1, keepdims=True) + 1e-06  1.43 us
  transfers between devices with their start and end apart: 14, of which 6 were waited for; matrix products, arithmetic and copies ran while one was open for 12% of the time, Pallas kernels for 0%

commit v1 on v0

v1 whole, which is shorter than its diff:
```python
import jax
import jax.numpy as jnp
from jax import lax
from jax.experimental import pallas as pl
from jax.experimental.pallas import tpu as pltpu
from jax.sharding import PartitionSpec as P


LANES = 128
FLOOR = -1.0


def normalize(embeddings):
    values = embeddings.astype(jnp.float32)
    inverse = lax.rsqrt(jnp.sum(values * values, axis=-1, keepdims=True) + 1e-06)
    return (values * inverse).astype(jnp.bfloat16)


def listed(lists, block, other):
    hit = lists[block, 0] == other
    for slot in range(1, lists.shape[1]):
        hit = jnp.logical_or(hit, lists[block, slot] == other)
    return hit


def as_column(order):
    return jnp.broadcast_to(order, (LANES, order.shape[1])).T


def sweep(units, order_col, other_units, other_order, lists_other, other_lists, want_cols, rows):
    after = jnp.where(lists_other, other_order, jnp.int32(2**30))
    before = jnp.where(other_lists, other_order, -1)
    col_early, col_late = [], []
    step = 2 * LANES
    for tile in range(0, other_units.shape[0], step):
        scores = lax.dot_general(
            units, other_units[tile : tile + step], (((1,), (1,)), ((), ())),
            preferred_element_type=jnp.float32,
        )
        for at in range(0, step, LANES):
            piece = scores[:, at : at + LANES]
            span = slice(tile + at, tile + at + LANES)
            down = jnp.where(after[:, span] < order_col, piece, FLOOR)
            up = jnp.where(order_col < before[:, span], piece, FLOOR)
            if want_cols:
                col_early.append(jnp.max(up, axis=0, keepdims=True))
                col_late.append(jnp.max(down, axis=0, keepdims=True))
            if rows is not None:
                rows[:] = [down, up] if not rows else [
                    jnp.maximum(rows[0], down), jnp.maximum(rows[1], up)
                ]
    if want_cols:
        return jnp.concatenate(col_early, axis=1), jnp.concatenate(col_late, axis=1)


def position():
    blocks = lax.axis_size("blk")
    here = lax.axis_index("blk")
    odd = here % 2
    partner = here + 1 - 2 * odd
    cross = (here + 2 + odd * (blocks - 4)) % blocks
    return here, partner, cross


def own_kernel(lists, e_ref, p_ref, o_order, p_order, uo_ref, up_ref, own_ref):
    here, partner, _ = position()
    uo_ref[...] = normalize(e_ref[...])
    up_ref[...] = normalize(p_ref[...])
    order = o_order[...]
    a = sweep(uo_ref[...], as_column(order), uo_ref, order, True, True, True, None)
    b = sweep(
        up_ref[...], as_column(p_order[...]), uo_ref, order,
        listed(lists, partner, here), listed(lists, here, partner), True, None,
    )
    for k in range(2):
        own_ref[k : k + 1, :] = jnp.maximum(a[k], b[k])


def cross_kernel(lists, r_ref, r_order, uo_ref, up_ref, o_order, p_order, own_ref, new_ref, ret_ref):
    here, partner, cross = position()
    ur = normalize(r_ref[...])
    order_r = as_column(r_order[...])
    rows = []
    cols = sweep(
        ur, order_r, uo_ref, o_order[...],
        listed(lists, cross, here), listed(lists, here, cross), True, rows,
    )
    sweep(
        ur, order_r, up_ref, p_order[...],
        listed(lists, cross, partner), listed(lists, partner, cross), False, rows,
    )
    for k in range(2):
        new_ref[k : k + 1, :] = jnp.maximum(own_ref[k : k + 1, :], cols[k])
        ret_ref[k : k + 1, :] = jnp.max(rows[k].T, axis=0, keepdims=True)


def last_kernel(own_ref, ret_ref, early_ref, late_ref):
    early_ref[...] = jnp.maximum(own_ref[0:1, :], ret_ref[0:1, :])
    late_ref[...] = jnp.maximum(own_ref[1:2, :], ret_ref[1:2, :]).astype(late_ref.dtype)


def call(kernel, outs, args, flops):
    specs = [pl.BlockSpec(memory_space=pltpu.VMEM)] * len(args)
    if args[0].dtype == jnp.int32:
        specs[0] = pl.BlockSpec(memory_space=pltpu.SMEM)
    return pl.pallas_call(
        kernel,
        out_shape=tuple(jax.ShapeDtypeStruct(s, d) for s, d in outs),
        in_specs=specs,
        out_specs=tuple(pl.BlockSpec(memory_space=pltpu.VMEM) for _ in outs),
        compiler_params=pltpu.CompilerParams(vmem_limit_bytes=24 * 2**20),
        cost_estimate=pl.CostEstimate(flops=flops, bytes_accessed=3 * 2**20, transcendentals=0),
    )(*args)


def steps(embeddings, doc_order, neighbours):
    rows, width = embeddings.shape
    blocks = lax.axis_size("blk")
    order = doc_order.reshape(1, rows)
    inner = [(i, i ^ 1) for i in range(blocks)]
    cross = [(i, (i + 2 if i % 2 else i - 2) % blocks) for i in range(blocks)]

    def send(x, pairs):
        return lax.ppermute(x, "blk", pairs)

    pair = ((2, rows), jnp.float32)
    unit = ((rows, width), jnp.bfloat16)
    work = 2 * rows * rows * width

    r = send(embeddings, cross)
    p = send(embeddings, inner)
    p_order = send(order, inner)
    r_order = send(order, cross)
    uo, up, own = call(
        own_kernel, (unit, unit, pair), (neighbours, embeddings, p, order, p_order), 2 * work
    )
    own, ret = call(
        cross_kernel, (pair, pair),
        (neighbours, r, r_order, uo, up, order, p_order, own), 2 * work,
    )
    ret = send(ret, [(j, i) for i, j in cross])
    early, late = call(
        last_kernel, (((1, rows), jnp.float32), ((1, rows), jnp.bfloat16)), (own, ret), 0
    )
    return early.reshape(rows), late.reshape(rows)


def solution(mesh):
    placed = (P(("groups", "blk"), None), P(("groups", "blk")), P("groups", None))
    return jax.shard_map(
        steps,
        mesh=mesh,
        in_specs=placed,
        out_specs=(P(("groups", "blk")), P(("groups", "blk"))),
        check_vma=False,
    )
```

time: 63.4 us -> 32.1 us (0.51)
  starting transfers between devices: 36.2 us -> 6.73 us
  matrix products: 6.25 us -> 0 us
  Pallas kernels: 0 us -> 4.68 us
  other arithmetic: 3.63 us -> 0.58 us
  local copies, waits for them, and re-layouts: 0.02 us -> 1.89 us
  waiting for transfers between devices: 16.3 us -> 17.4 us
    ppermute x14 -> x5, starting transfers between devices: 36.2 us -> 6.73 us  [send(): return lax.ppermute(x, 'blk', pairs)]
    dot_general x5 -> x0, matrix products: 6.25 us -> none  [pair_scores(): lax.dot_general(unit_rows, unit_cols, (((1,), (1,)), ((), ())), preferred...]
    pallas_call x0 -> x3, Pallas kernels: none -> 4.68 us  [call(): pl.pallas_call(kernel, out_shape=tuple((jax.ShapeDtypeStruct(s, d) for s,...]
    unnamed x6 -> x5, local copies, waits for them, and re-layouts: 0.01 us -> 1.89 us
    reduce_sum x1 -> x0, other arithmetic: 1.43 us -> none  [normalize(): jnp.sum(values * values, axis=-1, keepdims=True) + 1e-06]
    max x6 -> x0, other arithmetic: 1.18 us -> none  [the longest x1 0.58 us: visit(): jnp.maximum(row_best, jnp.max(masked, axis=1))]
    ppermute x14 -> x5, waiting for transfers between devices: 16.3 us -> 17.4 us  [send(): return lax.ppermute(x, 'blk', pairs)]
    reduce_or x1 -> x0, other arithmetic: 0.82 us -> none  [visit(): listed = jnp.any(my_list == block_id)]
  transfers between devices with their start and end apart: 14 -> 5, of which waited for: 6 -> 3; matrix products, arithmetic and copies ran while one was open for 12% -> 2% of each run, Pallas kernels for 0% -> 6%
where the time goes in v1:
time: 32.1 us; the launch traced here: 32 us
  waiting for transfers between devices  17.4 us (54%)
  starting transfers between devices  6.73 us (21%)
  Pallas kernels  4.68 us (15%)
  local copies, waits for them, and re-layouts  1.89 us (6%)
  between operations  0.65 us (2%)
  other arithmetic  0.58 us (2%)
    ppermute x5, waiting for transfers between devices, send(): return lax.ppermute(x, 'blk', pairs)  17.4 us
    ppermute x5, starting transfers between devices, send(): return lax.ppermute(x, 'blk', pairs)  6.73 us
    pallas_call x3, Pallas kernels, call(): pl.pallas_call(kernel, out_shape=tuple((jax.ShapeDtypeStruct(s, d) for s,...  4.68 us
    unnamed x5, local copies, waits for them, and re-layouts  1.89 us
  transfers between devices with their start and end apart: 5, of which 3 were waited for; matrix products, arithmetic and copies ran while one was open for 2% of the time, Pallas kernels for 6%

profile of v1, /device:TPU:0, one launch (start us, length us, event | category | flops | bytes accessed | tf_op | source)
XLA Modules:
  0.0 32.0 jit_solution(16851049812159802138)
XLA Ops:
  0.6 0.6 %collective-permute-start.2 = (bf16[512,768]{1,0:T(8,128)(2,1)}, bf16[512,768]{1,0:T(8,128)(2,1)S(1)}, u32[]{:S(2)}, u32[]{:S(2)}) collective-permute-start(bf16[512,768]{1,0:T(8,128)(2,1)} %e_ref.1), channel_id=1, source_target_pairs={{0,1},{1,0},{2,3},{3,2},{4,5},{5,4},{6,7},{7,6},{8,9},{9,8},{10,11... | collective-permute-start | bytes 2359304 | tf_op jit(solution)/shard_map/ppermute | solution.py:124
  1.2 5.6 %collective-permute-start = (bf16[512,768]{1,0:T(8,128)(2,1)}, bf16[512,768]{1,0:T(8,128)(2,1)S(1)}, u32[]{:S(2)}, u32[]{:S(2)}) collective-permute-start(bf16[512,768]{1,0:T(8,128)(2,1)} %e_ref.1), channel_id=1, source_target_pairs={{0,14},{1,3},{2,0},{3,5},{4,2},{5,7},{6,4},{7,9},{8,6},{9,11},{10,... | collective-permute-start | bytes 2359304 | tf_op jit(solution)/shard_map/ppermute | solution.py:124
  6.8 0.0 copy-start.1
  6.8 0.0 collective-permute-start.3
  6.8 0.5 %collective-permute-start.1 = (s32[1,512]{1,0:T(1,128)}, s32[1,512]{1,0:T(1,128)S(1)}, u32[]{:S(2)}, u32[]{:S(2)}) collective-permute-start(s32[1,512]{1,0:T(1,128)} %bitcast.3), channel_id=1, source_target_pairs={{0,14},{1,3},{2,0},{3,5},{4,2},{5,7},{6,4},{7,9},{8,6},{9,11},{10,... | collective-permute-start | bytes 6152 | tf_op jit(solution)/shard_map/ppermute | solution.py:124
  7.3 0.8 %copy.6.lists = s32[16,4]{1,0:T(8,128)S(1)} copy(s32[16,4]{0,1:T(4,128)} %param.5) | data formatting | bytes 512 | tf_op args[2]
  8.1 0.1 collective-permute-done.3.p_order
  8.2 0.0 collective-permute-done.2.p_ref
  8.2 0.0 copy-done.1
  8.2 0.0 copy-start
  8.2 1.1 %copy-done = bf16[512,768]{1,0:T(8,128)(2,1)S(1)} copy-done((bf16[512,768]{1,0:T(8,128)(2,1)S(1)}, bf16[512,768]{1,0:T(8,128)(2,1)}, u32[]{:S(2)}) %copy-start) | copy-done | bytes 786456
  9.3 2.1 %shard_map.50 = (bf16[512,768]{1,0:T(8,128)(2,1)S(1)}, bf16[512,768]{1,0:T(8,128)(2,1)S(1)}, f32[2,512]{1,0:T(2,128)S(1)}) custom-call(s32[16,4]{1,0:T(8,128)S(1)} %copy.6.lists, bf16[512,768]{1,0:T(8,128)(2,1)S(1)} %copy-done, bf16[512,768]{1,0:T(8,128)(2,1)S(1)} %collective-permute-done.2.p_ref, s32[1,512]{1,0:T(1,128)S(1)} %bitcast.4, ...), custom_call_target="tpu_custom_call" | custom-call | flops 805306368 | bytes 3145728 | tf_op jit(solution)/shard_map/pallas_call | solution.py:106
  11.4 11.0 %collective-permute-done.1.r_order = s32[1,512]{1,0:T(1,128)S(1)} collective-permute-done((s32[1,512]{1,0:T(1,128)}, s32[1,512]{1,0:T(1,128)S(1)}, u32[]{:S(2)}, u32[]{:S(2)}) %collective-permute-start.1) | collective-permute-done | bytes 2080 | tf_op jit(solution)/shard_map/ppermute | solution.py:124
  22.4 0.0 collective-permute-done.r_ref
  22.4 2.0 %shard_map.51 = (f32[2,512]{1,0:T(2,128)S(1)}, f32[2,512]{1,0:T(2,128)S(1)}) custom-call(s32[16,4]{1,0:T(8,128)S(1)} %copy.6.lists, bf16[512,768]{1,0:T(8,128)(2,1)S(1)} %collective-permute-done.r_ref, s32[1,512]{1,0:T(1,128)S(1)} %collective-permute-done.1.r_order, bf16[512,768]{1,0:T(8,128)(2,1)S(1)} %get-tuple-element.9.uo_ref, ...), custom_call_target="tpu_custom_call" | custom-call | flops 805306368 | bytes 3145728 | tf_op jit(solution)/shard_map/pallas_call | solution.py:106
  24.4 0.1 collective-permute-start.4
  24.5 6.3 %collective-permute-done.4.ret_ref = f32[2,512]{1,0:T(2,128)S(1)} collective-permute-done((f32[2,512]{1,0:T(2,128)S(1)}, f32[2,512]{1,0:T(2,128)S(1)}, u32[]{:S(2)}, u32[]{:S(2)}) %collective-permute-start.4) | collective-permute-done | bytes 4128 | tf_op jit(solution)/shard_map/ppermute | solution.py:124
  30.8 0.6 %shard_map.52 = (f32[1,512]{1,0:T(1,128)}, bf16[1,512]{1,0:T(2,128)(2,1)S(1)}) custom-call(f32[2,512]{1,0:T(2,128)S(1)} %get-tuple-element.12.own_ref, f32[2,512]{1,0:T(2,128)S(1)} %collective-permute-done.4.ret_ref), custom_call_target="tpu_custom_call" | custom-call | bytes 3145728 | tf_op jit(solution)/shard_map/pallas_call | solution.py:106
  31.4 0.6 %reduce = bf16[512]{0:T(512)(128)(2,1)} reduce(bf16[1,512]{1,0:T(2,128)(2,1)S(1)} %get-tuple-element.15, bf16[]{:T(256)} %constant), dimensions={0}, to_apply=%get-tuple-element.15.reduce_sub_computation | reduce | bytes 2050 | tf_op jit(solution)/shard_map/pallas_call | solution.py:106
Async XLA Ops:
  0.6 7.5 %collective-permute-start.2 = (bf16[512,768]{1,0:T(8,128)(2,1)}, bf16[512,768]{1,0:T(8,128)(2,1)S(1)}, u32[]{:S(2)}, u32[]{:S(2)}) collective-permute-start(bf16[512,768]{1,0:T(8,128)(2,1)} %e_ref.1), channel_id=1, source_target_pairs={{0,1},{1,0},{2,3},{3,2},{4,5},{5,4},{6,7},{7,6},{8,9},{9,8},{10,11... | collective-permute-start | bytes 2359304 | tf_op jit(solution)/shard_map/ppermute | solution.py:124
  1.2 21.2 %collective-permute-start = (bf16[512,768]{1,0:T(8,128)(2,1)}, bf16[512,768]{1,0:T(8,128)(2,1)S(1)}, u32[]{:S(2)}, u32[]{:S(2)}) collective-permute-start(bf16[512,768]{1,0:T(8,128)(2,1)} %e_ref.1), channel_id=1, source_target_pairs={{0,14},{1,3},{2,0},{3,5},{4,2},{5,7},{6,4},{7,9},{8,6},{9,11},{10,... | collective-permute-start | bytes 2359304 | tf_op jit(solution)/shard_map/ppermute | solution.py:124
  6.8 1.4 %copy-start.1 = (s32[512]{0:T(512)S(1)}, s32[512]{0:T(512)}, u32[]{:S(2)}) copy-start(s32[512]{0:T(512)} %param.4) | copy-start | bytes 6148
  6.8 1.4 %collective-permute-start.3 = (s32[1,512]{1,0:T(1,128)}, s32[1,512]{1,0:T(1,128)S(1)}, u32[]{:S(2)}, u32[]{:S(2)}) collective-permute-start(s32[1,512]{1,0:T(1,128)} %bitcast.2), channel_id=1, source_target_pairs={{0,1},{1,0},{2,3},{3,2},{4,5},{5,4},{6,7},{7,6},{8,9},{9,8},{10,11... | collective-permute-start | bytes 6152 | tf_op jit(solution)/shard_map/ppermute | solution.py:124
  6.8 15.6 %collective-permute-start.1 = (s32[1,512]{1,0:T(1,128)}, s32[1,512]{1,0:T(1,128)S(1)}, u32[]{:S(2)}, u32[]{:S(2)}) collective-permute-start(s32[1,512]{1,0:T(1,128)} %bitcast.3), channel_id=1, source_target_pairs={{0,14},{1,3},{2,0},{3,5},{4,2},{5,7},{6,4},{7,9},{8,6},{9,11},{10,... | collective-permute-start | bytes 6152 | tf_op jit(solution)/shard_map/ppermute | solution.py:124
  8.2 1.1 %copy-start = (bf16[512,768]{1,0:T(8,128)(2,1)S(1)}, bf16[512,768]{1,0:T(8,128)(2,1)}, u32[]{:S(2)}) copy-start(bf16[512,768]{1,0:T(8,128)(2,1)} %e_ref.1) | copy-start | bytes 2359300
  24.4 6.4 %collective-permute-start.4 = (f32[2,512]{1,0:T(2,128)S(1)}, f32[2,512]{1,0:T(2,128)S(1)}, u32[]{:S(2)}, u32[]{:S(2)}) collective-permute-start(f32[2,512]{1,0:T(2,128)S(1)} %get-tuple-element.13), channel_id=1, source_target_pairs={{14,0},{3,1},{0,2},{5,3},{2,4},{7,5},{4,6},{9,7},{6,8},{11,9},{8,1... | collective-permute-start | bytes 12296 | tf_op jit(solution)/shard_map/ppermute | solution.py:124

commit v2 on v1

--- a/solution.py
+++ b/solution.py
@@ -1,3 +1,5 @@
+import functools
+
 import jax
 import jax.numpy as jnp
 from jax import lax
@@ -59,11 +61,12 @@
     odd = here % 2
     partner = here + 1 - 2 * odd
     cross = (here + 2 + odd * (blocks - 4)) % blocks
-    return here, partner, cross
+    outer = (here % 4 == 0) | (here % 4 == 3)
+    return here, partner, cross, outer
 
 
 def own_kernel(lists, e_ref, p_ref, o_order, p_order, uo_ref, up_ref, own_ref):
-    here, partner, _ = position()
+    here, partner, _, _ = position()
     uo_ref[...] = normalize(e_ref[...])
     up_ref[...] = normalize(p_ref[...])
     order = o_order[...]
@@ -76,27 +79,39 @@
         own_ref[k : k + 1, :] = jnp.maximum(a[k], b[k])
 
 
-def cross_kernel(lists, r_ref, r_order, uo_ref, up_ref, o_order, p_order, own_ref, new_ref, ret_ref):
-    here, partner, cross = position()
-    ur = normalize(r_ref[...])
-    order_r = as_column(r_order[...])
-    rows = []
-    cols = sweep(
-        ur, order_r, uo_ref, o_order[...],
-        listed(lists, cross, here), listed(lists, here, cross), True, rows,
-    )
-    sweep(
-        ur, order_r, up_ref, p_order[...],
-        listed(lists, cross, partner), listed(lists, partner, cross), False, rows,
-    )
-    for k in range(2):
-        new_ref[k : k + 1, :] = jnp.maximum(own_ref[k : k + 1, :], cols[k])
-        ret_ref[k : k + 1, :] = jnp.max(rows[k].T, axis=0, keepdims=True)
+def cross_kernel(
+    on_outer, lists, r_ref, r_order, uo_ref, up_ref, o_order, p_order, own_ref, new_ref, ret_ref
+):
+    here, partner, cross, outer = position()
+
+    @pl.when(outer != on_outer)
+    def _():
+        new_ref[...] = own_ref[...]
+
+    @pl.when(outer == on_outer)
+    def _():
+        ur = normalize(r_ref[...])
+        order_r = as_column(r_order[...])
+        rows = []
+        cols = sweep(
+            ur, order_r, uo_ref, o_order[...],
+            listed(lists, cross, here), listed(lists, here, cross), True, rows,
+        )
+        sweep(
+            ur, order_r, up_ref, p_order[...],
+            listed(lists, cross, partner), listed(lists, partner, cross), False, rows,
+        )
+        for k in range(2):
+            new_ref[k : k + 1, :] = jnp.maximum(own_ref[k : k + 1, :], cols[k])
+            ret_ref[k : k + 1, :] = jnp.max(rows[k].T, axis=0, keepdims=True)
 
 
-def last_kernel(own_ref, ret_ref, early_ref, late_ref):
-    early_ref[...] = jnp.maximum(own_ref[0:1, :], ret_ref[0:1, :])
-    late_ref[...] = jnp.maximum(own_ref[1:2, :], ret_ref[1:2, :]).astype(late_ref.dtype)
+def last_kernel(own_ref, diag_ref, near_ref, early_ref, late_ref):
+    _, _, _, outer = position()
+    back = jnp.where(outer, diag_ref[...], near_ref[...])
+    best = jnp.maximum(own_ref[...], back)
+    early_ref[...] = best[0]
+    late_ref[...] = best[1].astype(late_ref.dtype)
 
 
 def call(kernel, outs, args, flops):
@@ -119,30 +134,42 @@
     order = doc_order.reshape(1, rows)
     inner = [(i, i ^ 1) for i in range(blocks)]
     cross = [(i, (i + 2 if i % 2 else i - 2) % blocks) for i in range(blocks)]
+    near = [(i, j) for i, j in cross if i % 4 in (1, 2)]
+    diag = [(i, j) for i, j in cross if i % 4 in (0, 3)]
 
     def send(x, pairs):
         return lax.ppermute(x, "blk", pairs)
+
+    def back(x, pairs):
+        return send(x, [(j, i) for i, j in pairs])
 
     pair = ((2, rows), jnp.float32)
     unit = ((rows, width), jnp.bfloat16)
     work = 2 * rows * rows * width
 
-    r = send(embeddings, cross)
+    e_near = send(embeddings, near)
+    e_diag = send(embeddings, diag)
+    o_diag = send(order, diag)
+    o_near = send(order, near)
     p = send(embeddings, inner)
     p_order = send(order, inner)
-    r_order = send(order, cross)
     uo, up, own = call(
         own_kernel, (unit, unit, pair), (neighbours, embeddings, p, order, p_order), 2 * work
     )
-    own, ret = call(
-        cross_kernel, (pair, pair),
-        (neighbours, r, r_order, uo, up, order, p_order, own), 2 * work,
+    own, ret_diag = call(
+        functools.partial(cross_kernel, False), (pair, pair),
+        (neighbours, e_diag, o_diag, uo, up, order, p_order, own), 2 * work,
     )
-    ret = send(ret, [(j, i) for i, j in cross])
-    early, late = call(
-        last_kernel, (((1, rows), jnp.float32), ((1, rows), jnp.bfloat16)), (own, ret), 0
+    ret_diag = back(ret_diag, diag)
+    own, ret_near = call(
+        functools.partial(cross_kernel, True), (pair, pair),
+        (neighbours, e_near, o_near, uo, up, order, p_order, own), 2 * work,
     )
-    return early.reshape(rows), late.reshape(rows)
+    ret_near = back(ret_near, near)
+    return call(
+        last_kernel, (((rows,), jnp.float32), ((rows,), jnp.bfloat16)),
+        (own, ret_diag, ret_near), 0,
+    )
 
 
 def solution(mesh):

time: 32.1 us -> 38.9 us (1.21)
  starting transfers between devices: 6.73 us -> 17.8 us
  waiting for transfers between devices: 17.4 us -> 12.8 us
  Pallas kernels: 4.68 us -> 5.44 us
  other arithmetic: 0.58 us -> 0 us
    ppermute x5 -> x8, starting transfers between devices: 6.73 us -> 17.8 us  [send(): return lax.ppermute(x, 'blk', pairs)]
    ppermute x5 -> x8, waiting for transfers between devices: 17.4 us -> 12.8 us  [send(): return lax.ppermute(x, 'blk', pairs)]
    pallas_call x3 -> x4, Pallas kernels: 4.68 us -> 5.44 us  [call(): pl.pallas_call(kernel, out_shape=tuple((jax.ShapeDtypeStruct(s, d) for s,...]
    pallas_call x1 -> x0, other arithmetic: 0.58 us -> none  [call(): pl.pallas_call(kernel, out_shape=tuple((jax.ShapeDtypeStruct(s, d) for s,...]
  transfers between devices with their start and end apart: 5 -> 8, of which waited for: 3 -> 2; matrix products, arithmetic and copies ran while one was open for 2% -> 2% of each run, Pallas kernels for 6% -> 7%
where the time goes in v2:
time: 38.9 us; the launch traced here: 38.6 us
  starting transfers between devices  17.8 us (46%)
  waiting for transfers between devices  12.8 us (33%)
  Pallas kernels  5.44 us (14%)
  local copies, waits for them, and re-layouts  1.89 us (5%)
  between operations  0.75 us (2%)
    ppermute x8, starting transfers between devices, send(): return lax.ppermute(x, 'blk', pairs)  17.8 us
    ppermute x8, waiting for transfers between devices, send(): return lax.ppermute(x, 'blk', pairs)  12.8 us
    pallas_call x4, Pallas kernels, call(): pl.pallas_call(kernel, out_shape=tuple((jax.ShapeDtypeStruct(s, d) for s,...  5.44 us
    unnamed x5, local copies, waits for them, and re-layouts  1.89 us
  transfers between devices with their start and end apart: 8, of which 2 were waited for; matrix products, arithmetic and copies ran while one was open for 2% of the time, Pallas kernels for 7%

profile of v2, /device:TPU:0, one launch (start us, length us, event | category | flops | bytes accessed | tf_op | source)
XLA Modules:
  0.0 38.6 jit_solution(429571522216664887)
XLA Ops:
  0.6 0.6 %collective-permute-start.2 = (bf16[512,768]{1,0:T(8,128)(2,1)}, bf16[512,768]{1,0:T(8,128)(2,1)S(1)}, u32[]{:S(2)}, u32[]{:S(2)}) collective-permute-start(bf16[512,768]{1,0:T(8,128)(2,1)} %e_ref.1), channel_id=1, source_target_pairs={{0,1},{1,0},{2,3},{3,2},{4,5},{5,4},{6,7},{7,6},{8,9},{9,8},{10,11... | collective-permute-start | bytes 2359304 | tf_op jit(solution)/shard_map/ppermute | solution.py:141
  1.2 7.5 %collective-permute-start.4 = (bf16[512,768]{1,0:T(8,128)(2,1)}, bf16[512,768]{1,0:T(8,128)(2,1)S(1)}, u32[]{:S(2)}, u32[]{:S(2)}) collective-permute-start(bf16[512,768]{1,0:T(8,128)(2,1)} %e_ref.1), channel_id=1, source_target_pairs={{0,14},{3,5},{4,2},{7,9},{8,6},{11,13},{12,10},{15,1},{16,30},{19,... | collective-permute-start | bytes 2359304 | tf_op jit(solution)/shard_map/ppermute | solution.py:141
  8.7 1.3 %collective-permute-start = (bf16[512,768]{1,0:T(8,128)(2,1)}, bf16[512,768]{1,0:T(8,128)(2,1)S(1)}, u32[]{:S(2)}, u32[]{:S(2)}) collective-permute-start(bf16[512,768]{1,0:T(8,128)(2,1)} %e_ref.1), channel_id=1, source_target_pairs={{1,3},{2,0},{5,7},{6,4},{9,11},{10,8},{13,15},{14,12},{17,19},{18,... | collective-permute-start | bytes 2359304 | tf_op jit(solution)/shard_map/ppermute | solution.py:141
  10.0 0.1 collective-permute-start.3
  10.1 4.5 %collective-permute-start.5 = (s32[1,512]{1,0:T(1,128)}, s32[1,512]{1,0:T(1,128)S(1)}, u32[]{:S(2)}, u32[]{:S(2)}) collective-permute-start(s32[1,512]{1,0:T(1,128)} %bitcast.2), channel_id=1, source_target_pairs={{0,14},{3,5},{4,2},{7,9},{8,6},{11,13},{12,10},{15,1},{16,30},{19,... | collective-permute-start | bytes 6152 | tf_op jit(solution)/shard_map/ppermute | solution.py:141
  14.6 0.8 %copy.7.lists = s32[16,4]{1,0:T(8,128)S(1)} copy(s32[16,4]{0,1:T(4,128)} %param.5) | data formatting | bytes 512 | tf_op args[2]
  15.3 0.0 collective-permute-done.3.p_order
  15.3 0.0 copy-done.1
  15.3 1.3 %collective-permute-start.1 = (s32[1,512]{1,0:T(1,128)S(1)}, s32[1,512]{1,0:T(1,128)S(1)}, u32[]{:S(2)}, u32[]{:S(2)}) collective-permute-start(s32[1,512]{1,0:T(1,128)S(1)} %bitcast.3), channel_id=1, source_target_pairs={{1,3},{2,0},{5,7},{6,4},{9,11},{10,8},{13,15},{14,12},{17,19},{18,... | collective-permute-start | bytes 6152 | tf_op jit(solution)/shard_map/ppermute | solution.py:141
  16.6 0.0 collective-permute-done.2.p_ref
  16.6 0.0 copy-start
  16.7 1.1 %copy-done = bf16[512,768]{1,0:T(8,128)(2,1)S(1)} copy-done((bf16[512,768]{1,0:T(8,128)(2,1)S(1)}, bf16[512,768]{1,0:T(8,128)(2,1)}, u32[]{:S(2)}) %copy-start) | copy-done | bytes 786456
  17.8 2.1 %shard_map.50 = (bf16[512,768]{1,0:T(8,128)(2,1)S(1)}, bf16[512,768]{1,0:T(8,128)(2,1)S(1)}, f32[2,512]{1,0:T(2,128)S(1)}) custom-call(s32[16,4]{1,0:T(8,128)S(1)} %copy.7.lists, bf16[512,768]{1,0:T(8,128)(2,1)S(1)} %copy-done, bf16[512,768]{1,0:T(8,128)(2,1)S(1)} %collective-permute-done.2.p_ref, s32[1,512]{1,0:T(1,128)S(1)} %bitcast.4, ...), custom_call_target="tpu_custom_call" | custom-call | flops 805306368 | bytes 3145728 | tf_op jit(solution)/shard_map/pallas_call | solution.py:121
  19.9 0.0 collective-permute-done.5.r_order
  19.9 0.0 collective-permute-done.4.r_ref
  19.9 0.7 %shard_map.51 = (f32[2,512]{1,0:T(2,128)S(1)}, f32[2,512]{1,0:T(2,128)S(1)}) custom-call(s32[16,4]{1,0:T(8,128)S(1)} %copy.7.lists, bf16[512,768]{1,0:T(8,128)(2,1)S(1)} %collective-permute-done.4.r_ref, s32[1,512]{1,0:T(1,128)S(1)} %collective-permute-done.5.r_order, bf16[512,768]{1,0:T(8,128)(2,1)S(1)} %get-tuple-element.9.uo_ref, ...), custom_call_target="tpu_custom_call" | custom-call | flops 805306368 | bytes 3145728 | tf_op jit(solution)/shard_map/pallas_call | solution.py:121
  20.6 5.9 %collective-permute-done.1.r_order = s32[1,512]{1,0:T(1,128)S(1)} collective-permute-done((s32[1,512]{1,0:T(1,128)S(1)}, s32[1,512]{1,0:T(1,128)S(1)}, u32[]{:S(2)}, u32[]{:S(2)}) %collective-permute-start.1) | collective-permute-done | bytes 2080 | tf_op jit(solution)/shard_map/ppermute | solution.py:141
  26.5 0.0 collective-permute-done.r_ref
  26.5 2.1 %shard_map.52 = (f32[2,512]{1,0:T(2,128)S(1)}, f32[2,512]{1,0:T(2,128)S(1)}) custom-call(s32[16,4]{1,0:T(8,128)S(1)} %copy.7.lists, bf16[512,768]{1,0:T(8,128)(2,1)S(1)} %collective-permute-done.r_ref, s32[1,512]{1,0:T(1,128)S(1)} %collective-permute-done.1.r_order, bf16[512,768]{1,0:T(8,128)(2,1)S(1)} %get-tuple-element.9.uo_ref, ...), custom_call_target="tpu_custom_call" | custom-call | flops 805306368 | bytes 3145728 | tf_op jit(solution)/shard_map/pallas_call | solution.py:121
  28.5 1.3 %collective-permute-start.7 = (f32[2,512]{1,0:T(2,128)S(1)}, f32[2,512]{1,0:T(2,128)S(1)}, u32[]{:S(2)}, u32[]{:S(2)}) collective-permute-start(f32[2,512]{1,0:T(2,128)S(1)} %get-tuple-element.15), channel_id=1, source_target_pairs={{3,1},{0,2},{7,5},{4,6},{11,9},{8,10},{15,13},{12,14},{19,17},{16,... | collective-permute-start | bytes 12296 | tf_op jit(solution)/shard_map/ppermute | solution.py:141
  29.8 1.3 %collective-permute-start.6 = (f32[2,512]{1,0:T(2,128)S(1)}, f32[2,512]{1,0:T(2,128)S(1)}, u32[]{:S(2)}, u32[]{:S(2)}) collective-permute-start(f32[2,512]{1,0:T(2,128)S(1)} %get-tuple-element.14), channel_id=1, source_target_pairs={{14,0},{5,3},{2,4},{9,7},{6,8},{13,11},{10,12},{1,15},{30,16},{21,... | collective-permute-start | bytes 12296 | tf_op jit(solution)/shard_map/ppermute | solution.py:141
  31.1 0.0 collective-permute-done.7.near_ref
  31.2 6.9 %collective-permute-done.6.diag_ref = f32[2,512]{1,0:T(2,128)S(1)} collective-permute-done((f32[2,512]{1,0:T(2,128)S(1)}, f32[2,512]{1,0:T(2,128)S(1)}, u32[]{:S(2)}, u32[]{:S(2)}) %collective-permute-start.6) | collective-permute-done | bytes 4128 | tf_op jit(solution)/shard_map/ppermute | solution.py:141
  38.0 0.6 %shard_map.53 = (f32[512]{0:T(512)}, bf16[512]{0:T(512)(128)(2,1)}) custom-call(f32[2,512]{1,0:T(2,128)S(1)} %get-tuple-element.13.own_ref, f32[2,512]{1,0:T(2,128)S(1)} %collective-permute-done.6.diag_ref, f32[2,512]{1,0:T(2,128)S(1)} %collective-permute-done.7.near_ref), custom_call_target="tpu_custom_call" | custom-call | bytes 3145728 | tf_op jit(solution)/shard_map/pallas_call | solution.py:121
  (1 shorter events, 0.0 us)
Async XLA Ops:
  0.6 16.0 %collective-permute-start.2 = (bf16[512,768]{1,0:T(8,128)(2,1)}, bf16[512,768]{1,0:T(8,128)(2,1)S(1)}, u32[]{:S(2)}, u32[]{:S(2)}) collective-permute-start(bf16[512,768]{1,0:T(8,128)(2,1)} %e_ref.1), channel_id=1, source_target_pairs={{0,1},{1,0},{2,3},{3,2},{4,5},{5,4},{6,7},{7,6},{8,9},{9,8},{10,11... | collective-permute-start | bytes 2359304 | tf_op jit(solution)/shard_map/ppermute | solution.py:141
  1.2 18.7 %collective-permute-start.4 = (bf16[512,768]{1,0:T(8,128)(2,1)}, bf16[512,768]{1,0:T(8,128)(2,1)S(1)}, u32[]{:S(2)}, u32[]{:S(2)}) collective-permute-start(bf16[512,768]{1,0:T(8,128)(2,1)} %e_ref.1), channel_id=1, source_target_pairs={{0,14},{3,5},{4,2},{7,9},{8,6},{11,13},{12,10},{15,1},{16,30},{19,... | collective-permute-start | bytes 2359304 | tf_op jit(solution)/shard_map/ppermute | solution.py:141
  8.7 17.8 %collective-permute-start = (bf16[512,768]{1,0:T(8,128)(2,1)}, bf16[512,768]{1,0:T(8,128)(2,1)S(1)}, u32[]{:S(2)}, u32[]{:S(2)}) collective-permute-start(bf16[512,768]{1,0:T(8,128)(2,1)} %e_ref.1), channel_id=1, source_target_pairs={{1,3},{2,0},{5,7},{6,4},{9,11},{10,8},{13,15},{14,12},{17,19},{18,... | collective-permute-start | bytes 2359304 | tf_op jit(solution)/shard_map/ppermute | solution.py:141
  10.0 5.3 %copy-start.1 = (s32[512]{0:T(512)S(1)}, s32[512]{0:T(512)}, u32[]{:S(2)}) copy-start(s32[512]{0:T(512)} %param.4) | copy-start | bytes 6148
  10.0 5.3 %collective-permute-start.3 = (s32[1,512]{1,0:T(1,128)}, s32[1,512]{1,0:T(1,128)S(1)}, u32[]{:S(2)}, u32[]{:S(2)}) collective-permute-start(s32[1,512]{1,0:T(1,128)} %bitcast.1), channel_id=1, source_target_pairs={{0,1},{1,0},{2,3},{3,2},{4,5},{5,4},{6,7},{7,6},{8,9},{9,8},{10,11... | collective-permute-start | bytes 6152 | tf_op jit(solution)/shard_map/ppermute | solution.py:141
  10.1 9.8 %collective-permute-start.5 = (s32[1,512]{1,0:T(1,128)}, s32[1,512]{1,0:T(1,128)S(1)}, u32[]{:S(2)}, u32[]{:S(2)}) collective-permute-start(s32[1,512]{1,0:T(1,128)} %bitcast.2), channel_id=1, source_target_pairs={{0,14},{3,5},{4,2},{7,9},{8,6},{11,13},{12,10},{15,1},{16,30},{19,... | collective-permute-start | bytes 6152 | tf_op jit(solution)/shard_map/ppermute | solution.py:141
  15.3 11.1 %collective-permute-start.1 = (s32[1,512]{1,0:T(1,128)S(1)}, s32[1,512]{1,0:T(1,128)S(1)}, u32[]{:S(2)}, u32[]{:S(2)}) collective-permute-start(s32[1,512]{1,0:T(1,128)S(1)} %bitcast.3), channel_id=1, source_target_pairs={{1,3},{2,0},{5,7},{6,4},{9,11},{10,8},{13,15},{14,12},{17,19},{18,... | collective-permute-start | bytes 6152 | tf_op jit(solution)/shard_map/ppermute | solution.py:141
  16.6 1.1 %copy-start = (bf16[512,768]{1,0:T(8,128)(2,1)S(1)}, bf16[512,768]{1,0:T(8,128)(2,1)}, u32[]{:S(2)}) copy-start(bf16[512,768]{1,0:T(8,128)(2,1)} %e_ref.1) | copy-start | bytes 2359300
  28.5 2.6 %collective-permute-start.7 = (f32[2,512]{1,0:T(2,128)S(1)}, f32[2,512]{1,0:T(2,128)S(1)}, u32[]{:S(2)}, u32[]{:S(2)}) collective-permute-start(f32[2,512]{1,0:T(2,128)S(1)} %get-tuple-element.15), channel_id=1, source_target_pairs={{3,1},{0,2},{7,5},{4,6},{11,9},{8,10},{15,13},{12,14},{19,17},{16,... | collective-permute-start | bytes 12296 | tf_op jit(solution)/shard_map/ppermute | solution.py:141
  29.8 8.2 %collective-permute-start.6 = (f32[2,512]{1,0:T(2,128)S(1)}, f32[2,512]{1,0:T(2,128)S(1)}, u32[]{:S(2)}, u32[]{:S(2)}) collective-permute-start(f32[2,512]{1,0:T(2,128)S(1)} %get-tuple-element.14), channel_id=1, source_target_pairs={{14,0},{5,3},{2,4},{9,7},{6,8},{13,11},{10,12},{1,15},{30,16},{21,... | collective-permute-start | bytes 12296 | tf_op jit(solution)/shard_map/ppermute | solution.py:141

commit v3 on v2

--- a/solution.py
+++ b/solution.py
@@ -29,9 +29,9 @@
     return jnp.broadcast_to(order, (LANES, order.shape[1])).T
 
 
-def sweep(units, order_col, other_units, other_order, lists_other, other_lists, want_cols, rows):
-    after = jnp.where(lists_other, other_order, jnp.int32(2**30))
-    before = jnp.where(other_lists, other_order, -1)
+def sweep(units, order_col, other_units, other_order, flags, want_cols, rows):
+    after = jnp.where(flags[0] > 0, other_order, jnp.int32(2**30))
+    before = jnp.where(flags[1] > 0, other_order, -1)
     col_early, col_late = [], []
     step = 2 * LANES
     for tile in range(0, other_units.shape[0], step):
@@ -61,55 +61,61 @@
     odd = here % 2
     partner = here + 1 - 2 * odd
     cross = (here + 2 + odd * (blocks - 4)) % blocks
-    outer = (here % 4 == 0) | (here % 4 == 3)
-    return here, partner, cross, outer
+    wraps = (here == 1) | (here == blocks - 2)
+    return here, partner, cross, wraps
 
 
-def own_kernel(lists, e_ref, p_ref, o_order, p_order, uo_ref, up_ref, own_ref):
-    here, partner, _, _ = position()
+def own_kernel(
+    lists, e_ref, p_ref, o_order, p_order, uo_ref, up_ref, own_ref, flag_ref
+):
+    here, partner, cross, _ = position()
+    pairs = ((cross, here), (here, cross), (cross, partner), (partner, cross),
+             (partner, here), (here, partner))
+    for k, (a, b) in enumerate(pairs):
+        flag = jnp.where(listed(lists, a, b), 1, 0)
+        flag_ref[k : k + 1, :] = jnp.broadcast_to(flag, (1, flag_ref.shape[1]))
     uo_ref[...] = normalize(e_ref[...])
     up_ref[...] = normalize(p_ref[...])
     order = o_order[...]
-    a = sweep(uo_ref[...], as_column(order), uo_ref, order, True, True, True, None)
+    always = jnp.ones_like(order)
+    a = sweep(uo_ref[...], as_column(order), uo_ref, order, (always, always), True, None)
     b = sweep(
         up_ref[...], as_column(p_order[...]), uo_ref, order,
-        listed(lists, partner, here), listed(lists, here, partner), True, None,
+        (flag_ref[4:5, :], flag_ref[5:6, :]), True, None,
     )
     for k in range(2):
         own_ref[k : k + 1, :] = jnp.maximum(a[k], b[k])
 
 
 def cross_kernel(
-    on_outer, lists, r_ref, r_order, uo_ref, up_ref, o_order, p_order, own_ref, new_ref, ret_ref
+    on_wrap, r_ref, r_order, uo_ref, up_ref, o_order, p_order, flag_ref, own_ref, new_ref, ret_ref
 ):
-    here, partner, cross, outer = position()
+    _, _, _, wraps = position()
 
-    @pl.when(outer != on_outer)
+    @pl.when(wraps != on_wrap)
     def _():
         new_ref[...] = own_ref[...]
 
-    @pl.when(outer == on_outer)
+    @pl.when(wraps == on_wrap)
     def _():
         ur = normalize(r_ref[...])
         order_r = as_column(r_order[...])
         rows = []
         cols = sweep(
-            ur, order_r, uo_ref, o_order[...],
-            listed(lists, cross, here), listed(lists, here, cross), True, rows,
+            ur, order_r, uo_ref, o_order[...], (flag_ref[0:1, :], flag_ref[1:2, :]), True, rows
         )
         sweep(
-            ur, order_r, up_ref, p_order[...],
-            listed(lists, cross, partner), listed(lists, partner, cross), False, rows,
+            ur, order_r, up_ref, p_order[...], (flag_ref[2:3, :], flag_ref[3:4, :]), False, rows
         )
         for k in range(2):
             new_ref[k : k + 1, :] = jnp.maximum(own_ref[k : k + 1, :], cols[k])
             ret_ref[k : k + 1, :] = jnp.max(rows[k].T, axis=0, keepdims=True)
 
 
-def last_kernel(own_ref, diag_ref, near_ref, early_ref, late_ref):
-    _, _, _, outer = position()
-    back = jnp.where(outer, diag_ref[...], near_ref[...])
-    best = jnp.maximum(own_ref[...], back)
+def last_kernel(own_ref, cross_ref, wrap_ref, early_ref, late_ref):
+    here = lax.axis_index("blk")
+    ends = (here == 0) | (here == lax.axis_size("blk") - 1)
+    best = jnp.maximum(own_ref[...], jnp.where(ends, wrap_ref[...], cross_ref[...]))
     early_ref[...] = best[0]
     late_ref[...] = best[1].astype(late_ref.dtype)
 
@@ -133,9 +139,8 @@
     blocks = lax.axis_size("blk")
     order = doc_order.reshape(1, rows)
     inner = [(i, i ^ 1) for i in range(blocks)]
-    cross = [(i, (i + 2 if i % 2 else i - 2) % blocks) for i in range(blocks)]
-    near = [(i, j) for i, j in cross if i % 4 in (1, 2)]
-    diag = [(i, j) for i, j in cross if i % 4 in (0, 3)]
+    cross = [(i, i + 2 if i % 2 else i - 2) for i in range(1, blocks - 1)]
+    wrap = [(0, blocks - 2), (blocks - 1, 1)]
 
     def send(x, pairs):
         return lax.ppermute(x, "blk", pairs)
@@ -145,30 +150,31 @@
 
     pair = ((2, rows), jnp.float32)
     unit = ((rows, width), jnp.bfloat16)
+    flags = ((6, rows), jnp.int32)
     work = 2 * rows * rows * width
 
-    e_near = send(embeddings, near)
-    e_diag = send(embeddings, diag)
-    o_diag = send(order, diag)
-    o_near = send(order, near)
+    e_cross = send(embeddings, cross)
+    e_wrap = send(embeddings, wrap)
+    o_wrap = send(order, wrap)
     p = send(embeddings, inner)
     p_order = send(order, inner)
-    uo, up, own = call(
-        own_kernel, (unit, unit, pair), (neighbours, embeddings, p, order, p_order), 2 * work
+    o_cross = send(order, cross)
+    uo, up, own, flag = call(
+        own_kernel, (unit, unit, pair, flags), (neighbours, embeddings, p, order, p_order), 2 * work
     )
-    own, ret_diag = call(
+    own, ret_wrap = call(
+        functools.partial(cross_kernel, True), (pair, pair),
+        (e_wrap, o_wrap, uo, up, order, p_order, flag, own), 2 * work,
+    )
+    ret_wrap = back(ret_wrap, wrap)
+    own, ret_cross = call(
         functools.partial(cross_kernel, False), (pair, pair),
-        (neighbours, e_diag, o_diag, uo, up, order, p_order, own), 2 * work,
+        (e_cross, o_cross, uo, up, order, p_order, flag, own), 2 * work,
     )
-    ret_diag = back(ret_diag, diag)
-    own, ret_near = call(
-        functools.partial(cross_kernel, True), (pair, pair),
-        (neighbours, e_near, o_near, uo, up, order, p_order, own), 2 * work,
-    )
-    ret_near = back(ret_near, near)
+    ret_cross = back(ret_cross, cross)
     return call(
         last_kernel, (((rows,), jnp.float32), ((rows,), jnp.bfloat16)),
-        (own, ret_diag, ret_near), 0,
+        (own, ret_cross, ret_wrap), 0,
     )
 
 

time: 38.9 us -> 38.5 us (0.990)
  waiting for transfers between devices: 12.8 us -> 16.1 us
  starting transfers between devices: 17.8 us -> 15.4 us
  Pallas kernels: 5.44 us -> 4.06 us
    ppermute x8, waiting for transfers between devices: 12.8 us -> 16.1 us  [send(): return lax.ppermute(x, 'blk', pairs)]
    ppermute x8, starting transfers between devices: 17.8 us -> 15.4 us  [send(): return lax.ppermute(x, 'blk', pairs)]
    pallas_call x4, Pallas kernels: 5.44 us -> 4.06 us  [call(): pl.pallas_call(kernel, out_shape=tuple((jax.ShapeDtypeStruct(s, d) for s,...]
  transfers between devices with their start and end apart: 8 -> 8, of which waited for: 2 -> 3; matrix products, arithmetic and copies ran while one was open for 2% -> 2% of each run, Pallas kernels for 7% -> 5%
where the time goes in v3:
time: 38.5 us; the launch traced here: 38.2 us
  waiting for transfers between devices  16.1 us (42%)
  starting transfers between devices  15.4 us (40%)
  Pallas kernels  4.06 us (11%)
  local copies, waits for them, and re-layouts  1.89 us (5%)
  between operations  0.72 us (2%)
    ppermute x8, waiting for transfers between devices, send(): return lax.ppermute(x, 'blk', pairs)  16.1 us
    ppermute x8, starting transfers between devices, send(): return lax.ppermute(x, 'blk', pairs)  15.4 us
    pallas_call x4, Pallas kernels, call(): pl.pallas_call(kernel, out_shape=tuple((jax.ShapeDtypeStruct(s, d) for s,...  4.06 us
    unnamed x5, local copies, waits for them, and re-layouts  1.89 us
  transfers between devices with their start and end apart: 8, of which 3 were waited for; matrix products, arithmetic and copies ran while one was open for 2% of the time, Pallas kernels for 5%

profile of v3, /device:TPU:0, one launch (start us, length us, event | category | flops | bytes accessed | tf_op | source)
XLA Modules:
  0.0 38.2 jit_solution(12342388705867850826)
XLA Ops:
  0.6 0.6 %collective-permute-start.2 = (bf16[512,768]{1,0:T(8,128)(2,1)}, bf16[512,768]{1,0:T(8,128)(2,1)S(1)}, u32[]{:S(2)}, u32[]{:S(2)}) collective-permute-start(bf16[512,768]{1,0:T(8,128)(2,1)} %e_ref.1), channel_id=1, source_target_pairs={{0,1},{1,0},{2,3},{3,2},{4,5},{5,4},{6,7},{7,6},{8,9},{9,8},{10,11... | collective-permute-start | bytes 2359304 | tf_op jit(solution)/shard_map/ppermute | solution.py:146
  1.2 7.5 %collective-permute-start.4 = (bf16[512,768]{1,0:T(8,128)(2,1)}, bf16[512,768]{1,0:T(8,128)(2,1)S(1)}, u32[]{:S(2)}, u32[]{:S(2)}) collective-permute-start(bf16[512,768]{1,0:T(8,128)(2,1)} %e_ref.1), channel_id=1, source_target_pairs={{0,14},{15,1},{16,30},{31,17}} | collective-permute-start | bytes 2359304 | tf_op jit(solution)/shard_map/ppermute | solution.py:146
  8.7 1.3 %collective-permute-start = (bf16[512,768]{1,0:T(8,128)(2,1)}, bf16[512,768]{1,0:T(8,128)(2,1)S(1)}, u32[]{:S(2)}, u32[]{:S(2)}) collective-permute-start(bf16[512,768]{1,0:T(8,128)(2,1)} %e_ref.1), channel_id=1, source_target_pairs={{1,3},{2,0},{3,5},{4,2},{5,7},{6,4},{7,9},{8,6},{9,11},{10,8},{11,... | collective-permute-start | bytes 2359304 | tf_op jit(solution)/shard_map/ppermute | solution.py:146
  10.0 0.0 copy-start.1
  10.0 0.1 collective-permute-start.3
  10.1 1.8 %collective-permute-start.5 = (s32[1,512]{1,0:T(1,128)}, s32[1,512]{1,0:T(1,128)S(1)}, u32[]{:S(2)}, u32[]{:S(2)}) collective-permute-start(s32[1,512]{1,0:T(1,128)} %bitcast.2), channel_id=1, source_target_pairs={{0,14},{15,1},{16,30},{31,17}} | collective-permute-start | bytes 6152 | tf_op jit(solution)/shard_map/ppermute | solution.py:146
  11.9 0.8 %copy.5.lists = s32[16,4]{1,0:T(8,128)S(1)} copy(s32[16,4]{0,1:T(4,128)} %param.5) | data formatting | bytes 512 | tf_op args[2]
  12.7 0.0 collective-permute-done.3.p_order
  12.7 0.0 copy-done.1
  12.7 1.3 %collective-permute-start.1 = (s32[1,512]{1,0:T(1,128)S(1)}, s32[1,512]{1,0:T(1,128)S(1)}, u32[]{:S(2)}, u32[]{:S(2)}) collective-permute-start(s32[1,512]{1,0:T(1,128)S(1)} %bitcast.3), channel_id=1, source_target_pairs={{1,3},{2,0},{3,5},{4,2},{5,7},{6,4},{7,9},{8,6},{9,11},{10,8},{11,... | collective-permute-start | bytes 6152 | tf_op jit(solution)/shard_map/ppermute | solution.py:146
  14.0 0.0 collective-permute-done.2.p_ref
  14.0 0.0 copy-start
  14.0 1.1 %copy-done = bf16[512,768]{1,0:T(8,128)(2,1)S(1)} copy-done((bf16[512,768]{1,0:T(8,128)(2,1)S(1)}, bf16[512,768]{1,0:T(8,128)(2,1)}, u32[]{:S(2)}) %copy-start) | copy-done | bytes 786456
  15.1 2.1 %shard_map.50 = (bf16[512,768]{1,0:T(8,128)(2,1)S(1)}, bf16[512,768]{1,0:T(8,128)(2,1)S(1)}, f32[2,512]{1,0:T(2,128)S(1)}, s32[6,512]{1,0:T(8,128)S(1)}) custom-call(s32[16,4]{1,0:T(8,128)S(1)} %copy.5.lists, bf16[512,768]{1,0:T(8,128)(2,1)S(1)} %copy-done, bf16[512,768]{1,0:T(8,128)(2,1)S(1)} %collective-permute-done.2.p_ref, s32[1,512]{1,0:T(1,128)S(1)} %bitcast.4, ...), custom_call_target="tpu_custom_call" | custom-call | flops 805306368 | bytes 3145728 | tf_op jit(solution)/shard_map/pallas_call | solution.py:127
  17.2 1.2 %collective-permute-done.5.r_order = s32[1,512]{1,0:T(1,128)S(1)} collective-permute-done((s32[1,512]{1,0:T(1,128)}, s32[1,512]{1,0:T(1,128)S(1)}, u32[]{:S(2)}, u32[]{:S(2)}) %collective-permute-start.5) | collective-permute-done | bytes 2080 | tf_op jit(solution)/shard_map/ppermute | solution.py:146
  18.5 0.0 collective-permute-done.4.r_ref
  18.5 8.0 %collective-permute-done.1.r_order = s32[1,512]{1,0:T(1,128)S(1)} collective-permute-done((s32[1,512]{1,0:T(1,128)S(1)}, s32[1,512]{1,0:T(1,128)S(1)}, u32[]{:S(2)}, u32[]{:S(2)}) %collective-permute-start.1) | collective-permute-done | bytes 2080 | tf_op jit(solution)/shard_map/ppermute | solution.py:146
  26.5 0.0 collective-permute-done.r_ref
  26.5 1.4 %shard_map.52 = (f32[2,512]{1,0:T(2,128)S(1)}, f32[2,512]{1,0:T(2,128)S(1)}) custom-call(bf16[512,768]{1,0:T(8,128)(2,1)S(1)} %collective-permute-done.r_ref, s32[1,512]{1,0:T(1,128)S(1)} %collective-permute-done.1.r_order, bf16[512,768]{1,0:T(8,128)(2,1)S(1)} %get-tuple-element.10.uo_ref, bf16[512,768]{1,0:T(8,128)(2,1)S(1)} %get-tuple-element.11.up_ref, ...), custom_call_target="tpu_custom_call" | custom-call | flops 805306368 | bytes 3145728 | tf_op jit(solution)/shard_map/pallas_call | solution.py:127
  27.9 1.5 %collective-permute-start.6 = (f32[2,512]{1,0:T(2,128)S(1)}, f32[2,512]{1,0:T(2,128)S(1)}, u32[]{:S(2)}, u32[]{:S(2)}) collective-permute-start(f32[2,512]{1,0:T(2,128)S(1)} %get-tuple-element.16), channel_id=1, source_target_pairs={{3,1},{0,2},{5,3},{2,4},{7,5},{4,6},{9,7},{6,8},{11,9},{8,10},{13,... | collective-permute-start | bytes 12296 | tf_op jit(solution)/shard_map/ppermute | solution.py:146
  29.4 1.3 %collective-permute-start.7 = (f32[2,512]{1,0:T(2,128)S(1)}, f32[2,512]{1,0:T(2,128)S(1)}, u32[]{:S(2)}, u32[]{:S(2)}) collective-permute-start(f32[2,512]{1,0:T(2,128)S(1)} %get-tuple-element.17), channel_id=1, source_target_pairs={{14,0},{1,15},{30,16},{17,31}} | collective-permute-start | bytes 12296 | tf_op jit(solution)/shard_map/ppermute | solution.py:146
  30.7 0.0 collective-permute-done.6.cross_ref
  30.7 6.9 %collective-permute-done.7.wrap_ref = f32[2,512]{1,0:T(2,128)S(1)} collective-permute-done((f32[2,512]{1,0:T(2,128)S(1)}, f32[2,512]{1,0:T(2,128)S(1)}, u32[]{:S(2)}, u32[]{:S(2)}) %collective-permute-start.7) | collective-permute-done | bytes 4128 | tf_op jit(solution)/shard_map/ppermute | solution.py:146
  37.6 0.6 %shard_map.53 = (f32[512]{0:T(512)}, bf16[512]{0:T(512)(128)(2,1)}) custom-call(f32[2,512]{1,0:T(2,128)S(1)} %get-tuple-element.15.own_ref, f32[2,512]{1,0:T(2,128)S(1)} %collective-permute-done.6.cross_ref, f32[2,512]{1,0:T(2,128)S(1)} %collective-permute-done.7.wrap_ref), custom_call_target="tpu_custom_call" | custom-call | bytes 3145728 | tf_op jit(solution)/shard_map/pallas_call | solution.py:127
  (1 shorter events, 0.0 us)
Async XLA Ops:
  0.6 13.4 %collective-permute-start.2 = (bf16[512,768]{1,0:T(8,128)(2,1)}, bf16[512,768]{1,0:T(8,128)(2,1)S(1)}, u32[]{:S(2)}, u32[]{:S(2)}) collective-permute-start(bf16[512,768]{1,0:T(8,128)(2,1)} %e_ref.1), channel_id=1, source_target_pairs={{0,1},{1,0},{2,3},{3,2},{4,5},{5,4},{6,7},{7,6},{8,9},{9,8},{10,11... | collective-permute-start | bytes 2359304 | tf_op jit(solution)/shard_map/ppermute | solution.py:146
  1.2 17.3 %collective-permute-start.4 = (bf16[512,768]{1,0:T(8,128)(2,1)}, bf16[512,768]{1,0:T(8,128)(2,1)S(1)}, u32[]{:S(2)}, u32[]{:S(2)}) collective-permute-start(bf16[512,768]{1,0:T(8,128)(2,1)} %e_ref.1), channel_id=1, source_target_pairs={{0,14},{15,1},{16,30},{31,17}} | collective-permute-start | bytes 2359304 | tf_op jit(solution)/shard_map/ppermute | solution.py:146
  8.7 17.8 %collective-permute-start = (bf16[512,768]{1,0:T(8,128)(2,1)}, bf16[512,768]{1,0:T(8,128)(2,1)S(1)}, u32[]{:S(2)}, u32[]{:S(2)}) collective-permute-start(bf16[512,768]{1,0:T(8,128)(2,1)} %e_ref.1), channel_id=1, source_target_pairs={{1,3},{2,0},{3,5},{4,2},{5,7},{6,4},{7,9},{8,6},{9,11},{10,8},{11,... | collective-permute-start | bytes 2359304 | tf_op jit(solution)/shard_map/ppermute | solution.py:146
  10.0 2.7 %copy-start.1 = (s32[512]{0:T(512)S(1)}, s32[512]{0:T(512)}, u32[]{:S(2)}) copy-start(s32[512]{0:T(512)} %param.4) | copy-start | bytes 6148
  10.0 2.7 %collective-permute-start.3 = (s32[1,512]{1,0:T(1,128)}, s32[1,512]{1,0:T(1,128)S(1)}, u32[]{:S(2)}, u32[]{:S(2)}) collective-permute-start(s32[1,512]{1,0:T(1,128)} %bitcast.1), channel_id=1, source_target_pairs={{0,1},{1,0},{2,3},{3,2},{4,5},{5,4},{6,7},{7,6},{8,9},{9,8},{10,11... | collective-permute-start | bytes 6152 | tf_op jit(solution)/shard_map/ppermute | solution.py:146
  10.1 8.4 %collective-permute-start.5 = (s32[1,512]{1,0:T(1,128)}, s32[1,512]{1,0:T(1,128)S(1)}, u32[]{:S(2)}, u32[]{:S(2)}) collective-permute-start(s32[1,512]{1,0:T(1,128)} %bitcast.2), channel_id=1, source_target_pairs={{0,14},{15,1},{16,30},{31,17}} | collective-permute-start | bytes 6152 | tf_op jit(solution)/shard_map/ppermute | solution.py:146
  12.7 13.8 %collective-permute-start.1 = (s32[1,512]{1,0:T(1,128)S(1)}, s32[1,512]{1,0:T(1,128)S(1)}, u32[]{:S(2)}, u32[]{:S(2)}) collective-permute-start(s32[1,512]{1,0:T(1,128)S(1)} %bitcast.3), channel_id=1, source_target_pairs={{1,3},{2,0},{3,5},{4,2},{5,7},{6,4},{7,9},{8,6},{9,11},{10,8},{11,... | collective-permute-start | bytes 6152 | tf_op jit(solution)/shard_map/ppermute | solution.py:146
  14.0 1.1 %copy-start = (bf16[512,768]{1,0:T(8,128)(2,1)S(1)}, bf16[512,768]{1,0:T(8,128)(2,1)}, u32[]{:S(2)}) copy-start(bf16[512,768]{1,0:T(8,128)(2,1)} %e_ref.1) | copy-start | bytes 2359300
  27.9 2.9 %collective-permute-start.6 = (f32[2,512]{1,0:T(2,128)S(1)}, f32[2,512]{1,0:T(2,128)S(1)}, u32[]{:S(2)}, u32[]{:S(2)}) collective-permute-start(f32[2,512]{1,0:T(2,128)S(1)} %get-tuple-element.16), channel_id=1, source_target_pairs={{3,1},{0,2},{5,3},{2,4},{7,5},{4,6},{9,7},{6,8},{11,9},{8,10},{13,... | collective-permute-start | bytes 12296 | tf_op jit(solution)/shard_map/ppermute | solution.py:146
  29.4 8.2 %collective-permute-start.7 = (f32[2,512]{1,0:T(2,128)S(1)}, f32[2,512]{1,0:T(2,128)S(1)}, u32[]{:S(2)}, u32[]{:S(2)}) collective-permute-start(f32[2,512]{1,0:T(2,128)S(1)} %get-tuple-element.17), channel_id=1, source_target_pairs={{14,0},{1,15},{30,16},{17,31}} | collective-permute-start | bytes 12296 | tf_op jit(solution)/shard_map/ppermute | solution.py:146

commit v4 on v3

--- a/solution.py
+++ b/solution.py
@@ -61,8 +61,8 @@
     odd = here % 2
     partner = here + 1 - 2 * odd
     cross = (here + 2 + odd * (blocks - 4)) % blocks
-    wraps = (here == 1) | (here == blocks - 2)
-    return here, partner, cross, wraps
+    outer = (here % 4 == 0) | (here % 4 == 3)
+    return here, partner, cross, outer
 
 
 def own_kernel(
@@ -88,15 +88,15 @@
 
 
 def cross_kernel(
-    on_wrap, r_ref, r_order, uo_ref, up_ref, o_order, p_order, flag_ref, own_ref, new_ref, ret_ref
+    on_outer, r_ref, r_order, uo_ref, up_ref, o_order, p_order, flag_ref, own_ref, new_ref, ret_ref
 ):
-    _, _, _, wraps = position()
+    _, _, _, outer = position()
 
-    @pl.when(wraps != on_wrap)
+    @pl.when(outer != on_outer)
     def _():
         new_ref[...] = own_ref[...]
 
-    @pl.when(wraps == on_wrap)
+    @pl.when(outer == on_outer)
     def _():
         ur = normalize(r_ref[...])
         order_r = as_column(r_order[...])
@@ -112,10 +112,9 @@
             ret_ref[k : k + 1, :] = jnp.max(rows[k].T, axis=0, keepdims=True)
 
 
-def last_kernel(own_ref, cross_ref, wrap_ref, early_ref, late_ref):
-    here = lax.axis_index("blk")
-    ends = (here == 0) | (here == lax.axis_size("blk") - 1)
-    best = jnp.maximum(own_ref[...], jnp.where(ends, wrap_ref[...], cross_ref[...]))
+def last_kernel(own_ref, diag_ref, near_ref, early_ref, late_ref):
+    _, _, _, outer = position()
+    best = jnp.maximum(own_ref[...], jnp.where(outer, diag_ref[...], near_ref[...]))
     early_ref[...] = best[0]
     late_ref[...] = best[1].astype(late_ref.dtype)
 
@@ -139,8 +138,9 @@
     blocks = lax.axis_size("blk")
     order = doc_order.reshape(1, rows)
     inner = [(i, i ^ 1) for i in range(blocks)]
-    cross = [(i, i + 2 if i % 2 else i - 2) for i in range(1, blocks - 1)]
-    wrap = [(0, blocks - 2), (blocks - 1, 1)]
+    cross = [(i, (i + 2 if i % 2 else i - 2) % blocks) for i in range(blocks)]
+    near = [cross[i] if i % 4 in (1, 2) else inner[i] for i in range(blocks)]
+    diag = [cross[i] if i % 4 in (0, 3) else inner[i] for i in range(blocks)]
 
     def send(x, pairs):
         return lax.ppermute(x, "blk", pairs)
@@ -153,28 +153,28 @@
     flags = ((6, rows), jnp.int32)
     work = 2 * rows * rows * width
 
-    e_cross = send(embeddings, cross)
-    e_wrap = send(embeddings, wrap)
-    o_wrap = send(order, wrap)
+    e_near = send(embeddings, near)
+    e_diag = send(embeddings, diag)
+    o_diag = send(order, diag)
     p = send(embeddings, inner)
     p_order = send(order, inner)
-    o_cross = send(order, cross)
+    o_near = send(order, near)
     uo, up, own, flag = call(
         own_kernel, (unit, unit, pair, flags), (neighbours, embeddings, p, order, p_order), 2 * work
     )
-    own, ret_wrap = call(
+    own, ret_diag = call(
+        functools.partial(cross_kernel, False), (pair, pair),
+        (e_diag, o_diag, uo, up, order, p_order, flag, own), 2 * work,
+    )
+    ret_diag = back(ret_diag, diag)
+    own, ret_near = call(
         functools.partial(cross_kernel, True), (pair, pair),
-        (e_wrap, o_wrap, uo, up, order, p_order, flag, own), 2 * work,
+        (e_near, o_near, uo, up, order, p_order, flag, own), 2 * work,
     )
-    ret_wrap = back(ret_wrap, wrap)
-    own, ret_cross = call(
-        functools.partial(cross_kernel, False), (pair, pair),
-        (e_cross, o_cross, uo, up, order, p_order, flag, own), 2 * work,
-    )
-    ret_cross = back(ret_cross, cross)
+    ret_near = back(ret_near, near)
     return call(
         last_kernel, (((rows,), jnp.float32), ((rows,), jnp.bfloat16)),
-        (own, ret_cross, ret_wrap), 0,
+        (own, ret_diag, ret_near), 0,
     )
 
 

time: 38.5 us -> 33.8 us (0.88)
  starting transfers between devices: 15.4 us -> 8.61 us
  waiting for transfers between devices: 16.1 us -> 18.3 us
    ppermute x8, starting transfers between devices: 15.4 us -> 8.61 us  [send(): return lax.ppermute(x, 'blk', pairs)]
    ppermute x8, waiting for transfers between devices: 16.1 us -> 18.3 us  [send(): return lax.ppermute(x, 'blk', pairs)]
  transfers between devices with their start and end apart: 8 -> 8, of which waited for: 3 -> 4; matrix products, arithmetic and copies ran while one was open for 2% -> 2% of each run, Pallas kernels for 5% -> 6%
where the time goes in v4:
time: 33.8 us; the launch traced here: 33.6 us
  waiting for transfers between devices  18.3 us (54%)
  starting transfers between devices  8.61 us (25%)
  Pallas kernels  4.06 us (12%)
  local copies, waits for them, and re-layouts  1.89 us (6%)
  between operations  0.68 us (2%)
    ppermute x8, waiting for transfers between devices, send(): return lax.ppermute(x, 'blk', pairs)  18.3 us
    ppermute x8, starting transfers between devices, send(): return lax.ppermute(x, 'blk', pairs)  8.61 us
    pallas_call x4, Pallas kernels, call(): pl.pallas_call(kernel, out_shape=tuple((jax.ShapeDtypeStruct(s, d) for s,...  4.06 us
    unnamed x5, local copies, waits for them, and re-layouts  1.89 us
  transfers between devices with their start and end apart: 8, of which 4 were waited for; matrix products, arithmetic and copies ran while one was open for 2% of the time, Pallas kernels for 6%

profile of v4, /device:TPU:0, one launch (start us, length us, event | category | flops | bytes accessed | tf_op | source)
XLA Modules:
  0.0 33.6 jit_solution(6289507833934213402)
XLA Ops:
  0.6 0.6 %collective-permute-start.2 = (bf16[512,768]{1,0:T(8,128)(2,1)}, bf16[512,768]{1,0:T(8,128)(2,1)S(1)}, u32[]{:S(2)}, u32[]{:S(2)}) collective-permute-start(bf16[512,768]{1,0:T(8,128)(2,1)} %e_ref.1), channel_id=1, source_target_pairs={{0,1},{1,0},{2,3},{3,2},{4,5},{5,4},{6,7},{7,6},{8,9},{9,8},{10,11... | collective-permute-start | bytes 2359304 | tf_op jit(solution)/shard_map/ppermute | solution.py:146
  1.2 5.6 %collective-permute-start.4 = (bf16[512,768]{1,0:T(8,128)(2,1)}, bf16[512,768]{1,0:T(8,128)(2,1)S(1)}, u32[]{:S(2)}, u32[]{:S(2)}) collective-permute-start(bf16[512,768]{1,0:T(8,128)(2,1)} %e_ref.1), channel_id=1, source_target_pairs={{0,14},{1,0},{2,3},{3,5},{4,2},{5,4},{6,7},{7,9},{8,6},{9,8},{10,1... | collective-permute-start | bytes 2359304 | tf_op jit(solution)/shard_map/ppermute | solution.py:146
  6.8 0.0 collective-permute-start
  6.8 0.0 copy-start.1
  6.8 0.0 collective-permute-start.3
  6.8 1.9 %collective-permute-start.5 = (s32[1,512]{1,0:T(1,128)}, s32[1,512]{1,0:T(1,128)S(1)}, u32[]{:S(2)}, u32[]{:S(2)}) collective-permute-start(s32[1,512]{1,0:T(1,128)} %bitcast.2), channel_id=1, source_target_pairs={{0,14},{1,0},{2,3},{3,5},{4,2},{5,4},{6,7},{7,9},{8,6},{9,8},{10,1... | collective-permute-start | bytes 6152 | tf_op jit(solution)/shard_map/ppermute | solution.py:146
  8.7 0.8 %copy.5.lists = s32[16,4]{1,0:T(8,128)S(1)} copy(s32[16,4]{0,1:T(4,128)} %param.5) | data formatting | bytes 512 | tf_op args[2]
  9.5 0.0 collective-permute-done.3.p_order
  9.5 0.0 copy-done.1
  9.5 0.0 collective-permute-start.1
  9.5 0.0 collective-permute-done.2.p_ref
  9.5 0.0 copy-start
  9.5 1.1 %copy-done = bf16[512,768]{1,0:T(8,128)(2,1)S(1)} copy-done((bf16[512,768]{1,0:T(8,128)(2,1)S(1)}, bf16[512,768]{1,0:T(8,128)(2,1)}, u32[]{:S(2)}) %copy-start) | copy-done | bytes 786456
  10.6 2.1 %shard_map.50 = (bf16[512,768]{1,0:T(8,128)(2,1)S(1)}, bf16[512,768]{1,0:T(8,128)(2,1)S(1)}, f32[2,512]{1,0:T(2,128)S(1)}, s32[6,512]{1,0:T(8,128)S(1)}) custom-call(s32[16,4]{1,0:T(8,128)S(1)} %copy.5.lists, bf16[512,768]{1,0:T(8,128)(2,1)S(1)} %copy-done, bf16[512,768]{1,0:T(8,128)(2,1)S(1)} %collective-permute-done.2.p_ref, s32[1,512]{1,0:T(1,128)S(1)} %bitcast.4, ...), custom_call_target="tpu_custom_call" | custom-call | flops 805306368 | bytes 3145728 | tf_op jit(solution)/shard_map/pallas_call | solution.py:126
  12.7 3.9 %collective-permute-done.5.r_order = s32[1,512]{1,0:T(1,128)S(1)} collective-permute-done((s32[1,512]{1,0:T(1,128)}, s32[1,512]{1,0:T(1,128)S(1)}, u32[]{:S(2)}, u32[]{:S(2)}) %collective-permute-start.5) | collective-permute-done | bytes 2080 | tf_op jit(solution)/shard_map/ppermute | solution.py:146
  16.6 0.0 collective-permute-done.4.r_ref
  16.6 8.6 %collective-permute-done.1.r_order = s32[1,512]{1,0:T(1,128)S(1)} collective-permute-done((s32[1,512]{1,0:T(1,128)S(1)}, s32[1,512]{1,0:T(1,128)S(1)}, u32[]{:S(2)}, u32[]{:S(2)}) %collective-permute-start.1) | collective-permute-done | bytes 2080 | tf_op jit(solution)/shard_map/ppermute | solution.py:146
  25.2 0.0 collective-permute-done.r_ref
  25.2 1.4 %shard_map.52 = (f32[2,512]{1,0:T(2,128)S(1)}, f32[2,512]{1,0:T(2,128)S(1)}) custom-call(bf16[512,768]{1,0:T(8,128)(2,1)S(1)} %collective-permute-done.r_ref, s32[1,512]{1,0:T(1,128)S(1)} %collective-permute-done.1.r_order, bf16[512,768]{1,0:T(8,128)(2,1)S(1)} %get-tuple-element.10.uo_ref, bf16[512,768]{1,0:T(8,128)(2,1)S(1)} %get-tuple-element.11.up_ref, ...), custom_call_target="tpu_custom_call" | custom-call | flops 805306368 | bytes 3145728 | tf_op jit(solution)/shard_map/pallas_call | solution.py:126
  26.6 0.0 collective-permute-start.7
  26.6 0.5 %collective-permute-start.6 = (f32[2,512]{1,0:T(2,128)S(1)}, f32[2,512]{1,0:T(2,128)S(1)}, u32[]{:S(2)}, u32[]{:S(2)}) collective-permute-start(f32[2,512]{1,0:T(2,128)S(1)} %get-tuple-element.16), channel_id=1, source_target_pairs={{14,0},{0,1},{3,2},{5,3},{2,4},{4,5},{7,6},{9,7},{6,8},{8,9},{11,1... | collective-permute-start | bytes 12296 | tf_op jit(solution)/shard_map/ppermute | solution.py:146
  27.1 0.8 %collective-permute-done.7.near_ref = f32[2,512]{1,0:T(2,128)S(1)} collective-permute-done((f32[2,512]{1,0:T(2,128)S(1)}, f32[2,512]{1,0:T(2,128)S(1)}, u32[]{:S(2)}, u32[]{:S(2)}) %collective-permute-start.7) | collective-permute-done | bytes 4128 | tf_op jit(solution)/shard_map/ppermute | solution.py:146
  27.9 5.0 %collective-permute-done.6.diag_ref = f32[2,512]{1,0:T(2,128)S(1)} collective-permute-done((f32[2,512]{1,0:T(2,128)S(1)}, f32[2,512]{1,0:T(2,128)S(1)}, u32[]{:S(2)}, u32[]{:S(2)}) %collective-permute-start.6) | collective-permute-done | bytes 4128 | tf_op jit(solution)/shard_map/ppermute | solution.py:146
  33.0 0.6 %shard_map.53 = (f32[512]{0:T(512)}, bf16[512]{0:T(512)(128)(2,1)}) custom-call(f32[2,512]{1,0:T(2,128)S(1)} %get-tuple-element.15.own_ref, f32[2,512]{1,0:T(2,128)S(1)} %collective-permute-done.6.diag_ref, f32[2,512]{1,0:T(2,128)S(1)} %collective-permute-done.7.near_ref), custom_call_target="tpu_custom_call" | custom-call | bytes 3145728 | tf_op jit(solution)/shard_map/pallas_call | solution.py:126
  (1 shorter events, 0.0 us)
Async XLA Ops:
  0.6 8.9 %collective-permute-start.2 = (bf16[512,768]{1,0:T(8,128)(2,1)}, bf16[512,768]{1,0:T(8,128)(2,1)S(1)}, u32[]{:S(2)}, u32[]{:S(2)}) collective-permute-start(bf16[512,768]{1,0:T(8,128)(2,1)} %e_ref.1), channel_id=1, source_target_pairs={{0,1},{1,0},{2,3},{3,2},{4,5},{5,4},{6,7},{7,6},{8,9},{9,8},{10,11... | collective-permute-start | bytes 2359304 | tf_op jit(solution)/shard_map/ppermute | solution.py:146
  1.2 15.4 %collective-permute-start.4 = (bf16[512,768]{1,0:T(8,128)(2,1)}, bf16[512,768]{1,0:T(8,128)(2,1)S(1)}, u32[]{:S(2)}, u32[]{:S(2)}) collective-permute-start(bf16[512,768]{1,0:T(8,128)(2,1)} %e_ref.1), channel_id=1, source_target_pairs={{0,14},{1,0},{2,3},{3,5},{4,2},{5,4},{6,7},{7,9},{8,6},{9,8},{10,1... | collective-permute-start | bytes 2359304 | tf_op jit(solution)/shard_map/ppermute | solution.py:146
  6.8 18.4 %collective-permute-start = (bf16[512,768]{1,0:T(8,128)(2,1)}, bf16[512,768]{1,0:T(8,128)(2,1)S(1)}, u32[]{:S(2)}, u32[]{:S(2)}) collective-permute-start(bf16[512,768]{1,0:T(8,128)(2,1)} %e_ref.1), channel_id=1, source_target_pairs={{0,1},{1,3},{2,0},{3,2},{4,5},{5,7},{6,4},{7,6},{8,9},{9,11},{10,8... | collective-permute-start | bytes 2359304 | tf_op jit(solution)/shard_map/ppermute | solution.py:146
  6.8 2.7 %copy-start.1 = (s32[512]{0:T(512)S(1)}, s32[512]{0:T(512)}, u32[]{:S(2)}) copy-start(s32[512]{0:T(512)} %param.4) | copy-start | bytes 6148
  6.8 2.7 %collective-permute-start.3 = (s32[1,512]{1,0:T(1,128)}, s32[1,512]{1,0:T(1,128)S(1)}, u32[]{:S(2)}, u32[]{:S(2)}) collective-permute-start(s32[1,512]{1,0:T(1,128)} %bitcast.1), channel_id=1, source_target_pairs={{0,1},{1,0},{2,3},{3,2},{4,5},{5,4},{6,7},{7,6},{8,9},{9,8},{10,11... | collective-permute-start | bytes 6152 | tf_op jit(solution)/shard_map/ppermute | solution.py:146
  6.8 9.8 %collective-permute-start.5 = (s32[1,512]{1,0:T(1,128)}, s32[1,512]{1,0:T(1,128)S(1)}, u32[]{:S(2)}, u32[]{:S(2)}) collective-permute-start(s32[1,512]{1,0:T(1,128)} %bitcast.2), channel_id=1, source_target_pairs={{0,14},{1,0},{2,3},{3,5},{4,2},{5,4},{6,7},{7,9},{8,6},{9,8},{10,1... | collective-permute-start | bytes 6152 | tf_op jit(solution)/shard_map/ppermute | solution.py:146
  9.5 15.7 %collective-permute-start.1 = (s32[1,512]{1,0:T(1,128)S(1)}, s32[1,512]{1,0:T(1,128)S(1)}, u32[]{:S(2)}, u32[]{:S(2)}) collective-permute-start(s32[1,512]{1,0:T(1,128)S(1)} %bitcast.3), channel_id=1, source_target_pairs={{0,1},{1,3},{2,0},{3,2},{4,5},{5,7},{6,4},{7,6},{8,9},{9,11},{10,8... | collective-permute-start | bytes 6152 | tf_op jit(solution)/shard_map/ppermute | solution.py:146
  9.5 1.1 %copy-start = (bf16[512,768]{1,0:T(8,128)(2,1)S(1)}, bf16[512,768]{1,0:T(8,128)(2,1)}, u32[]{:S(2)}) copy-start(bf16[512,768]{1,0:T(8,128)(2,1)} %e_ref.1) | copy-start | bytes 2359300
  26.6 1.4 %collective-permute-start.7 = (f32[2,512]{1,0:T(2,128)S(1)}, f32[2,512]{1,0:T(2,128)S(1)}, u32[]{:S(2)}, u32[]{:S(2)}) collective-permute-start(f32[2,512]{1,0:T(2,128)S(1)} %get-tuple-element.17), channel_id=1, source_target_pairs={{1,0},{3,1},{0,2},{2,3},{5,4},{7,5},{4,6},{6,7},{9,8},{11,9},{8,10... | collective-permute-start | bytes 12296 | tf_op jit(solution)/shard_map/ppermute | solution.py:146
  26.6 6.4 %collective-permute-start.6 = (f32[2,512]{1,0:T(2,128)S(1)}, f32[2,512]{1,0:T(2,128)S(1)}, u32[]{:S(2)}, u32[]{:S(2)}) collective-permute-start(f32[2,512]{1,0:T(2,128)S(1)} %get-tuple-element.16), channel_id=1, source_target_pairs={{14,0},{0,1},{3,2},{5,3},{2,4},{4,5},{7,6},{9,7},{6,8},{8,9},{11,1... | collective-permute-start | bytes 12296 | tf_op jit(solution)/shard_map/ppermute | solution.py:146

commit v5 on v4

--- a/solution.py
+++ b/solution.py
@@ -1,5 +1,3 @@
-import functools
-
 import jax
 import jax.numpy as jnp
 from jax import lax
@@ -9,6 +7,7 @@
 
 
 LANES = 128
+STRIP = 32
 FLOOR = -1.0
 
 
@@ -66,7 +65,7 @@
 
 
 def own_kernel(
-    lists, e_ref, p_ref, o_order, p_order, uo_ref, up_ref, own_ref, flag_ref
+    lists, e_ref, p_ref, o_order, p_order, uo_ref, up_ref, own_ref, flag_ref, ocol_ref, pcol_ref
 ):
     here, partner, cross, _ = position()
     pairs = ((cross, here), (here, cross), (cross, partner), (partner, cross),
@@ -78,48 +77,124 @@
     up_ref[...] = normalize(p_ref[...])
     order = o_order[...]
     always = jnp.ones_like(order)
-    a = sweep(uo_ref[...], as_column(order), uo_ref, order, (always, always), True, None)
+    ocol_ref[...] = as_column(order)
+    pcol_ref[...] = as_column(p_order[...])
+    a = sweep(uo_ref[...], ocol_ref[...], uo_ref, order, (always, always), True, None)
     b = sweep(
-        up_ref[...], as_column(p_order[...]), uo_ref, order,
+        up_ref[...], pcol_ref[...], uo_ref, order,
         (flag_ref[4:5, :], flag_ref[5:6, :]), True, None,
     )
     for k in range(2):
         own_ref[k : k + 1, :] = jnp.maximum(a[k], b[k])
 
 
-def cross_kernel(
-    on_outer, r_ref, r_order, uo_ref, up_ref, o_order, p_order, flag_ref, own_ref, new_ref, ret_ref
+def fold(x):
+    best = x[0:8]
+    for at in range(8, x.shape[0], 8):
+        best = jnp.maximum(best, x[at : at + 8])
+    return best
+
+
+def arrive(r_ref, r_order, held, flag_ref, ret_ref):
+    units = normalize(r_ref[...])
+    order = r_order[...]
+    rows = r_ref.shape[0]
+    best = [None, None]
+    for held_ref, col_ref, flag, acc_ref in held:
+        scores = lax.dot_general(
+            held_ref[...], units, (((1,), (1,)), ((), ())), preferred_element_type=jnp.float32
+        )
+        run = [[None] * (rows // LANES) for _ in range(2)]
+        for at in range(0, rows, STRIP):
+            col = col_ref[at : at + STRIP, :]
+            wide = [None, None]
+            for tile in range(rows // LANES):
+                span = slice(tile * LANES, tile * LANES + LANES)
+                piece = scores[at : at + STRIP, span]
+                after = order[:, span] > col
+                parts = (jnp.where(after, piece, FLOOR), jnp.where(after, FLOOR, piece))
+                for k in range(2):
+                    small = fold(parts[k])
+                    run[k][tile] = (
+                        small if run[k][tile] is None else jnp.maximum(run[k][tile], small)
+                    )
+                    if acc_ref is not None:
+                        wide[k] = parts[k] if wide[k] is None else jnp.maximum(wide[k], parts[k])
+            if acc_ref is not None:
+                acc_ref[at : at + STRIP, :] = wide[1]
+                acc_ref[rows + at : rows + at + STRIP, :] = wide[0]
+        for k in range(2):
+            line = jnp.concatenate([jnp.max(x, axis=0, keepdims=True) for x in run[k]], axis=1)
+            line = jnp.where(flag_ref[flag + k : flag + k + 1, :] > 0, line, FLOOR)
+            best[k] = line if best[k] is None else jnp.maximum(best[k], line)
+    for k in range(2):
+        ret_ref[k : k + 1, :] = best[k]
+
+
+def settle(acc_ref, flag_ref, flag):
+    rows = acc_ref.shape[0] // 2
+    lines = []
+    for k in range(2):
+        line = jnp.max(acc_ref[k * rows : k * rows + rows, :].T, axis=0, keepdims=True)
+        lines.append(jnp.where(flag_ref[flag + 1 - k : flag + 2 - k, :] > 0, line, FLOOR))
+    return lines
+
+
+def diag_kernel(
+    r_ref, r_order, uo_ref, up_ref, ocol_ref, pcol_ref, flag_ref, ret_ref, acc_ref, partner_ref,
+    pacc_ref,
+):
+    role = lax.axis_index("blk") % 4
+
+    @pl.when(role == 2)
+    def _():
+        arrive(r_ref, r_order, ((uo_ref, ocol_ref, 0, acc_ref),), flag_ref, ret_ref)
+
+    @pl.when(role == 1)
+    def _():
+        held = ((uo_ref, ocol_ref, 0, acc_ref), (up_ref, pcol_ref, 2, pacc_ref))
+        arrive(r_ref, r_order, held, flag_ref, ret_ref)
+        for k, line in enumerate(settle(pacc_ref, flag_ref, 2)):
+            partner_ref[k : k + 1, :] = line
+
+
+def near_kernel(
+    r_ref, r_order, uo_ref, up_ref, ocol_ref, pcol_ref, flag_ref, ret_ref, acc_ref
 ):
     _, _, _, outer = position()
 
-    @pl.when(outer != on_outer)
-    def _():
-        new_ref[...] = own_ref[...]
-
-    @pl.when(outer == on_outer)
-    def _():
-        ur = normalize(r_ref[...])
-        order_r = as_column(r_order[...])
-        rows = []
-        cols = sweep(
-            ur, order_r, uo_ref, o_order[...], (flag_ref[0:1, :], flag_ref[1:2, :]), True, rows
-        )
-        sweep(
-            ur, order_r, up_ref, p_order[...], (flag_ref[2:3, :], flag_ref[3:4, :]), False, rows
-        )
-        for k in range(2):
-            new_ref[k : k + 1, :] = jnp.maximum(own_ref[k : k + 1, :], cols[k])
-            ret_ref[k : k + 1, :] = jnp.max(rows[k].T, axis=0, keepdims=True)
-
-
-def last_kernel(own_ref, diag_ref, near_ref, early_ref, late_ref):
+    @pl.when(outer)
+    def _():
+        held = ((uo_ref, ocol_ref, 0, acc_ref), (up_ref, pcol_ref, 2, None))
+        arrive(r_ref, r_order, held, flag_ref, ret_ref)
+
+
+def own_last_kernel(own_ref, near_acc, diag_acc, flag_ref, new_ref):
+    _, _, _, outer = position()
+
+    def put(acc_ref):
+        for k, line in enumerate(settle(acc_ref, flag_ref, 0)):
+            new_ref[k : k + 1, :] = jnp.maximum(own_ref[k : k + 1, :], line)
+
+    @pl.when(outer)
+    def _():
+        put(near_acc)
+
+    @pl.when(jnp.logical_not(outer))
+    def _():
+        put(diag_acc)
+
+
+def last_kernel(own_ref, diag_ref, near_ref, partner_ref, early_ref, late_ref):
+    role = lax.axis_index("blk") % 4
     _, _, _, outer = position()
     best = jnp.maximum(own_ref[...], jnp.where(outer, diag_ref[...], near_ref[...]))
+    best = jnp.maximum(best, jnp.where(role == 0, partner_ref[...], FLOOR))
     early_ref[...] = best[0]
     late_ref[...] = best[1].astype(late_ref.dtype)
 
 
-def call(kernel, outs, args, flops):
+def call(kernel, outs, args, flops, scratch=()):
     specs = [pl.BlockSpec(memory_space=pltpu.VMEM)] * len(args)
     if args[0].dtype == jnp.int32:
         specs[0] = pl.BlockSpec(memory_space=pltpu.SMEM)
@@ -128,6 +203,7 @@
         out_shape=tuple(jax.ShapeDtypeStruct(s, d) for s, d in outs),
         in_specs=specs,
         out_specs=tuple(pl.BlockSpec(memory_space=pltpu.VMEM) for _ in outs),
+        scratch_shapes=scratch,
         compiler_params=pltpu.CompilerParams(vmem_limit_bytes=24 * 2**20),
         cost_estimate=pl.CostEstimate(flops=flops, bytes_accessed=3 * 2**20, transcendentals=0),
     )(*args)
@@ -159,22 +235,26 @@
     p = send(embeddings, inner)
     p_order = send(order, inner)
     o_near = send(order, near)
-    uo, up, own, flag = call(
-        own_kernel, (unit, unit, pair, flags), (neighbours, embeddings, p, order, p_order), 2 * work
-    )
-    own, ret_diag = call(
-        functools.partial(cross_kernel, False), (pair, pair),
-        (e_diag, o_diag, uo, up, order, p_order, flag, own), 2 * work,
+    col = ((rows, LANES), jnp.int32)
+    acc = ((2 * rows, LANES), jnp.float32)
+    uo, up, own, flag, ocol, pcol = call(
+        own_kernel, (unit, unit, pair, flags, col, col),
+        (neighbours, embeddings, p, order, p_order), 2 * work,
+    )
+    ret_diag, acc_diag, partner = call(
+        diag_kernel, (pair, acc, pair), (e_diag, o_diag, uo, up, ocol, pcol, flag), 2 * work,
+        (pltpu.VMEM(*acc),),
     )
     ret_diag = back(ret_diag, diag)
-    own, ret_near = call(
-        functools.partial(cross_kernel, True), (pair, pair),
-        (e_near, o_near, uo, up, order, p_order, flag, own), 2 * work,
+    partner = send(partner, inner)
+    ret_near, acc_near = call(
+        near_kernel, (pair, acc), (e_near, o_near, uo, up, ocol, pcol, flag), 2 * work
     )
     ret_near = back(ret_near, near)
+    (own,) = call(own_last_kernel, (pair,), (own, acc_near, acc_diag, flag), work)
     return call(
         last_kernel, (((rows,), jnp.float32), ((rows,), jnp.bfloat16)),
-        (own, ret_diag, ret_near), 0,
+        (own, ret_diag, ret_near, partner), 0,
     )
 
 

time: 33.8 us -> 28.7 us (0.85)
  waiting for transfers between devices: 18.3 us -> 12 us
  starting transfers between devices: 8.61 us -> 9.74 us
    ppermute x8 -> x9, waiting for transfers between devices: 18.3 us -> 12 us  [send(): return lax.ppermute(x, 'blk', pairs)]
    ppermute x8 -> x9, starting transfers between devices: 8.61 us -> 9.74 us  [send(): return lax.ppermute(x, 'blk', pairs)]
    pallas_call x4 -> x5, Pallas kernels: 4.06 us -> 4.18 us  [call(): pl.pallas_call(kernel, out_shape=tuple((jax.ShapeDtypeStruct(s, d) for s,...]
  transfers between devices with their start and end apart: 8 -> 9, of which waited for: 4 -> 3; matrix products, arithmetic and copies ran while one was open for 2% -> 3% of each run, Pallas kernels for 6% -> 13%
where the time goes in v5:
time: 28.7 us; the launch traced here: 28.5 us
  waiting for transfers between devices  12 us (42%)
  starting transfers between devices  9.74 us (34%)
  Pallas kernels  4.18 us (15%)
  local copies, waits for them, and re-layouts  1.89 us (7%)
  between operations  0.71 us (2%)
    ppermute x9, waiting for transfers between devices, send(): return lax.ppermute(x, 'blk', pairs)  12 us
    ppermute x9, starting transfers between devices, send(): return lax.ppermute(x, 'blk', pairs)  9.74 us
    pallas_call x5, Pallas kernels, call(): pl.pallas_call(kernel, out_shape=tuple((jax.ShapeDtypeStruct(s, d) for s,...  4.18 us
    unnamed x5, local copies, waits for them, and re-layouts  1.89 us
  transfers between devices with their start and end apart: 9, of which 3 were waited for; matrix products, arithmetic and copies ran while one was open for 3% of the time, Pallas kernels for 13%

profile of v5, /device:TPU:0, one launch (start us, length us, event | category | flops | bytes accessed | tf_op | source)
XLA Modules:
  0.0 28.5 jit_solution(1507365653836553263)
XLA Ops:
  0.6 0.6 %collective-permute-start = (bf16[512,768]{1,0:T(8,128)(2,1)}, bf16[512,768]{1,0:T(8,128)(2,1)S(1)}, u32[]{:S(2)}, u32[]{:S(2)}) collective-permute-start(bf16[512,768]{1,0:T(8,128)(2,1)} %e_ref.1), channel_id=1, source_target_pairs={{0,1},{1,0},{2,3},{3,2},{4,5},{5,4},{6,7},{7,6},{8,9},{9,8},{10,11... | collective-permute-start | bytes 2359304 | tf_op jit(solution)/shard_map/ppermute | solution.py:222
  1.2 5.6 %collective-permute-start.4 = (bf16[512,768]{1,0:T(8,128)(2,1)}, bf16[512,768]{1,0:T(8,128)(2,1)S(1)}, u32[]{:S(2)}, u32[]{:S(2)}) collective-permute-start(bf16[512,768]{1,0:T(8,128)(2,1)} %e_ref.1), channel_id=1, source_target_pairs={{0,14},{1,0},{2,3},{3,5},{4,2},{5,4},{6,7},{7,9},{8,6},{9,8},{10,1... | collective-permute-start | bytes 2359304 | tf_op jit(solution)/shard_map/ppermute | solution.py:222
  6.8 0.0 collective-permute-start.2
  6.8 0.0 collective-permute-start.1
  6.8 1.9 %collective-permute-start.5 = (s32[1,512]{1,0:T(1,128)}, s32[1,512]{1,0:T(1,128)S(1)}, u32[]{:S(2)}, u32[]{:S(2)}) collective-permute-start(s32[1,512]{1,0:T(1,128)} %bitcast.2), channel_id=1, source_target_pairs={{0,14},{1,0},{2,3},{3,5},{4,2},{5,4},{6,7},{7,9},{8,6},{9,8},{10,1... | collective-permute-start | bytes 6152 | tf_op jit(solution)/shard_map/ppermute | solution.py:222
  8.7 0.8 %copy.5.lists = s32[16,4]{1,0:T(8,128)S(1)} copy(s32[16,4]{0,1:T(4,128)} %param.5) | data formatting | bytes 512 | tf_op args[2]
  9.5 0.0 collective-permute-done.1.p_order
  9.5 0.0 collective-permute-start.3
  9.5 0.0 collective-permute-done.p_ref
  9.5 0.0 copy-start
  9.5 1.1 %copy-done = bf16[512,768]{1,0:T(8,128)(2,1)S(1)} copy-done((bf16[512,768]{1,0:T(8,128)(2,1)S(1)}, bf16[512,768]{1,0:T(8,128)(2,1)}, u32[]{:S(2)}) %copy-start) | copy-done | bytes 786456
  10.6 2.1 %shard_map.50 = (bf16[512,768]{1,0:T(8,128)(2,1)S(1)}, bf16[512,768]{1,0:T(8,128)(2,1)S(1)}, f32[2,512]{1,0:T(2,128)S(1)}, s32[6,512]{1,0:T(8,128)S(1)}, s32[512,128]{1,0:T(8,128)S(1)}, /*index=5*/s32[512,128]{1,0:T(8,128)S(1)}) custom-call(s32[16,4]{1,0:T(8,128)S(1)} %copy.5.lists, bf16[512,768]{1,0:T(8,128)(2,1)S(1)} %copy-done, ...), custom_call_target="tpu_custom_call" | custom-call | flops 805306368 | bytes 3145728 | tf_op jit(solution)/shard_map/pallas_call | solution.py:201
  12.7 3.9 %collective-permute-done.5.r_order = s32[1,512]{1,0:T(1,128)S(1)} collective-permute-done((s32[1,512]{1,0:T(1,128)}, s32[1,512]{1,0:T(1,128)S(1)}, u32[]{:S(2)}, u32[]{:S(2)}) %collective-permute-start.5) | collective-permute-done | bytes 2080 | tf_op jit(solution)/shard_map/ppermute | solution.py:222
  16.6 0.0 collective-permute-done.4.r_ref
  16.6 1.5 %collective-permute-start.6 = (f32[2,512]{1,0:T(2,128)S(1)}, f32[2,512]{1,0:T(2,128)S(1)}, u32[]{:S(2)}, u32[]{:S(2)}) collective-permute-start(f32[2,512]{1,0:T(2,128)S(1)} %get-tuple-element.21), channel_id=1, source_target_pairs={{14,0},{0,1},{3,2},{5,3},{2,4},{4,5},{7,6},{9,7},{6,8},{8,9},{11,1... | collective-permute-start | bytes 12296 | tf_op jit(solution)/shard_map/ppermute | solution.py:222
  18.2 0.1 collective-permute-start.8
  18.3 7.0 %collective-permute-done.3.r_order = s32[1,512]{1,0:T(1,128)S(1)} collective-permute-done((s32[1,512]{1,0:T(1,128)S(1)}, s32[1,512]{1,0:T(1,128)S(1)}, u32[]{:S(2)}, u32[]{:S(2)}) %collective-permute-start.3) | collective-permute-done | bytes 2080 | tf_op jit(solution)/shard_map/ppermute | solution.py:222
  25.2 0.0 collective-permute-done.2.r_ref
  25.2 1.3 %shard_map.51 = (f32[2,512]{1,0:T(2,128)S(1)}, f32[1024,128]{1,0:T(8,128)S(1)}) custom-call(bf16[512,768]{1,0:T(8,128)(2,1)S(1)} %collective-permute-done.2.r_ref, s32[1,512]{1,0:T(1,128)S(1)} %collective-permute-done.3.r_order, bf16[512,768]{1,0:T(8,128)(2,1)S(1)} %get-tuple-element.14.uo_ref, bf16[512,768]{1,0:T(8,128)(2,1)S(1)} %get-tuple-element.15.up_ref, ...), custom_call_target="tpu_custom_call" | custom-call | flops 805306368 | bytes 3145728 | tf_op jit(solution)/shard_map/pallas_call | solution.py:201
  26.5 0.0 collective-permute-start.7
  26.6 0.2 shard_map.53.own_ref
  26.8 0.0 collective-permute-done.6.diag_ref
  26.8 1.1 %collective-permute-done.7.near_ref = f32[2,512]{1,0:T(2,128)S(1)} collective-permute-done((f32[2,512]{1,0:T(2,128)S(1)}, f32[2,512]{1,0:T(2,128)S(1)}, u32[]{:S(2)}, u32[]{:S(2)}) %collective-permute-start.7) | collective-permute-done | bytes 4128 | tf_op jit(solution)/shard_map/ppermute | solution.py:222
  27.9 0.6 %shard_map.54 = (f32[512]{0:T(512)}, bf16[512]{0:T(512)(128)(2,1)}) custom-call(f32[2,512]{1,0:T(2,128)S(1)} %shard_map.53.own_ref, f32[2,512]{1,0:T(2,128)S(1)} %collective-permute-done.6.diag_ref, f32[2,512]{1,0:T(2,128)S(1)} %collective-permute-done.7.near_ref, f32[2,512]{1,0:T(2,128)S(1)} %collective-permute-done.8.partner_ref), custom_call_target="tpu_custom_call" | custom-call | bytes 3145728 | tf_op jit(solution)/shard_map/pallas_call | solution.py:201
  (4 shorter events, 0.0 us)
Async XLA Ops:
  0.6 8.9 %collective-permute-start = (bf16[512,768]{1,0:T(8,128)(2,1)}, bf16[512,768]{1,0:T(8,128)(2,1)S(1)}, u32[]{:S(2)}, u32[]{:S(2)}) collective-permute-start(bf16[512,768]{1,0:T(8,128)(2,1)} %e_ref.1), channel_id=1, source_target_pairs={{0,1},{1,0},{2,3},{3,2},{4,5},{5,4},{6,7},{7,6},{8,9},{9,8},{10,11... | collective-permute-start | bytes 2359304 | tf_op jit(solution)/shard_map/ppermute | solution.py:222
  1.2 15.4 %collective-permute-start.4 = (bf16[512,768]{1,0:T(8,128)(2,1)}, bf16[512,768]{1,0:T(8,128)(2,1)S(1)}, u32[]{:S(2)}, u32[]{:S(2)}) collective-permute-start(bf16[512,768]{1,0:T(8,128)(2,1)} %e_ref.1), channel_id=1, source_target_pairs={{0,14},{1,0},{2,3},{3,5},{4,2},{5,4},{6,7},{7,9},{8,6},{9,8},{10,1... | collective-permute-start | bytes 2359304 | tf_op jit(solution)/shard_map/ppermute | solution.py:222
  6.8 18.4 %collective-permute-start.2 = (bf16[512,768]{1,0:T(8,128)(2,1)}, bf16[512,768]{1,0:T(8,128)(2,1)S(1)}, u32[]{:S(2)}, u32[]{:S(2)}) collective-permute-start(bf16[512,768]{1,0:T(8,128)(2,1)} %e_ref.1), channel_id=1, source_target_pairs={{0,1},{1,3},{2,0},{3,2},{4,5},{5,7},{6,4},{7,6},{8,9},{9,11},{10,8... | collective-permute-start | bytes 2359304 | tf_op jit(solution)/shard_map/ppermute | solution.py:222
  6.8 2.7 %copy-start.1 = (s32[512]{0:T(512)S(1)}, s32[512]{0:T(512)}, u32[]{:S(2)}) copy-start(s32[512]{0:T(512)} %param.4) | copy-start | bytes 6148
  6.8 2.7 %collective-permute-start.1 = (s32[1,512]{1,0:T(1,128)}, s32[1,512]{1,0:T(1,128)S(1)}, u32[]{:S(2)}, u32[]{:S(2)}) collective-permute-start(s32[1,512]{1,0:T(1,128)} %bitcast.1), channel_id=1, source_target_pairs={{0,1},{1,0},{2,3},{3,2},{4,5},{5,4},{6,7},{7,6},{8,9},{9,8},{10,11... | collective-permute-start | bytes 6152 | tf_op jit(solution)/shard_map/ppermute | solution.py:222
  6.8 9.8 %collective-permute-start.5 = (s32[1,512]{1,0:T(1,128)}, s32[1,512]{1,0:T(1,128)S(1)}, u32[]{:S(2)}, u32[]{:S(2)}) collective-permute-start(s32[1,512]{1,0:T(1,128)} %bitcast.2), channel_id=1, source_target_pairs={{0,14},{1,0},{2,3},{3,5},{4,2},{5,4},{6,7},{7,9},{8,6},{9,8},{10,1... | collective-permute-start | bytes 6152 | tf_op jit(solution)/shard_map/ppermute | solution.py:222
  9.5 15.8 %collective-permute-start.3 = (s32[1,512]{1,0:T(1,128)S(1)}, s32[1,512]{1,0:T(1,128)S(1)}, u32[]{:S(2)}, u32[]{:S(2)}) collective-permute-start(s32[1,512]{1,0:T(1,128)S(1)} %bitcast.3), channel_id=1, source_target_pairs={{0,1},{1,3},{2,0},{3,2},{4,5},{5,7},{6,4},{7,6},{8,9},{9,11},{10,8... | collective-permute-start | bytes 6152 | tf_op jit(solution)/shard_map/ppermute | solution.py:222
  9.5 1.1 %copy-start = (bf16[512,768]{1,0:T(8,128)(2,1)S(1)}, bf16[512,768]{1,0:T(8,128)(2,1)}, u32[]{:S(2)}) copy-start(bf16[512,768]{1,0:T(8,128)(2,1)} %e_ref.1) | copy-start | bytes 2359300
  16.6 10.2 %collective-permute-start.6 = (f32[2,512]{1,0:T(2,128)S(1)}, f32[2,512]{1,0:T(2,128)S(1)}, u32[]{:S(2)}, u32[]{:S(2)}) collective-permute-start(f32[2,512]{1,0:T(2,128)S(1)} %get-tuple-element.21), channel_id=1, source_target_pairs={{14,0},{0,1},{3,2},{5,3},{2,4},{4,5},{7,6},{9,7},{6,8},{8,9},{11,1... | collective-permute-start | bytes 12296 | tf_op jit(solution)/shard_map/ppermute | solution.py:222
  18.2 8.6 %collective-permute-start.8 = (f32[2,512]{1,0:T(2,128)S(1)}, f32[2,512]{1,0:T(2,128)S(1)}, u32[]{:S(2)}, u32[]{:S(2)}) collective-permute-start(f32[2,512]{1,0:T(2,128)S(1)} %get-tuple-element.23), channel_id=1, source_target_pairs={{0,1},{1,0},{2,3},{3,2},{4,5},{5,4},{6,7},{7,6},{8,9},{9,8},{10,11... | collective-permute-start | bytes 12296 | tf_op jit(solution)/shard_map/ppermute | solution.py:222
  26.5 1.4 %collective-permute-start.7 = (f32[2,512]{1,0:T(2,128)S(1)}, f32[2,512]{1,0:T(2,128)S(1)}, u32[]{:S(2)}, u32[]{:S(2)}) collective-permute-start(f32[2,512]{1,0:T(2,128)S(1)} %get-tuple-element.22), channel_id=1, source_target_pairs={{1,0},{3,1},{0,2},{2,3},{5,4},{7,5},{4,6},{6,7},{9,8},{11,9},{8,10... | collective-permute-start | bytes 12296 | tf_op jit(solution)/shard_map/ppermute | solution.py:222

commit v6 on v5

--- a/solution.py
+++ b/solution.py
@@ -28,10 +28,10 @@
     return jnp.broadcast_to(order, (LANES, order.shape[1])).T
 
 
-def sweep(units, order_col, other_units, other_order, flags, want_cols, rows):
+def sweep(units, order_col, other_units, other_order, flags):
     after = jnp.where(flags[0] > 0, other_order, jnp.int32(2**30))
     before = jnp.where(flags[1] > 0, other_order, -1)
-    col_early, col_late = [], []
+    early, late = [], []
     step = 2 * LANES
     for tile in range(0, other_units.shape[0], step):
         scores = lax.dot_general(
@@ -41,35 +41,38 @@
         for at in range(0, step, LANES):
             piece = scores[:, at : at + LANES]
             span = slice(tile + at, tile + at + LANES)
+            up = jnp.where(order_col < before[:, span], piece, FLOOR)
             down = jnp.where(after[:, span] < order_col, piece, FLOOR)
-            up = jnp.where(order_col < before[:, span], piece, FLOOR)
-            if want_cols:
-                col_early.append(jnp.max(up, axis=0, keepdims=True))
-                col_late.append(jnp.max(down, axis=0, keepdims=True))
-            if rows is not None:
-                rows[:] = [down, up] if not rows else [
-                    jnp.maximum(rows[0], down), jnp.maximum(rows[1], up)
-                ]
-    if want_cols:
-        return jnp.concatenate(col_early, axis=1), jnp.concatenate(col_late, axis=1)
+            early.append(jnp.max(up, axis=0, keepdims=True))
+            late.append(jnp.max(down, axis=0, keepdims=True))
+    return jnp.concatenate(early, axis=1), jnp.concatenate(late, axis=1)
 
 
 def position():
     blocks = lax.axis_size("blk")
     here = lax.axis_index("blk")
-    odd = here % 2
-    partner = here + 1 - 2 * odd
-    cross = (here + 2 + odd * (blocks - 4)) % blocks
-    outer = (here % 4 == 0) | (here % 4 == 3)
-    return here, partner, cross, outer
+    return blocks, here, here % 4
+
+
+def tables(blocks):
+    inner = [i ^ 1 for i in range(blocks)]
+    near = [i + (1, 2, -2, -1)[i % 4] for i in range(blocks)]
+    diag = [(i + (-2, -1, 1, 2)[i % 4]) % blocks for i in range(blocks)]
+    diag[0], diag[blocks - 2] = blocks - 1, blocks - 2
+    return tuple(list(enumerate(table)) for table in (inner, near, diag))
 
 
 def own_kernel(
     lists, e_ref, p_ref, o_order, p_order, uo_ref, up_ref, own_ref, flag_ref, ocol_ref, pcol_ref
 ):
-    here, partner, cross, _ = position()
-    pairs = ((cross, here), (here, cross), (cross, partner), (partner, cross),
-             (partner, here), (here, partner))
+    blocks, here, role = position()
+    partner = here + 1 - 2 * (here % 2)
+    diag = jnp.where(role == 1, here + blocks - 2, here + 2) % blocks
+    diag = jnp.where(here == blocks - 1, 0, diag)
+    near = jnp.where(role == 0, here + 2, here + blocks - 2) % blocks
+    pairs = []
+    for a, b in ((diag, here), (diag, partner), (near, here), (near, partner), (partner, here)):
+        pairs += [(a, b), (b, a)]
     for k, (a, b) in enumerate(pairs):
         flag = jnp.where(listed(lists, a, b), 1, 0)
         flag_ref[k : k + 1, :] = jnp.broadcast_to(flag, (1, flag_ref.shape[1]))
@@ -79,10 +82,9 @@
     always = jnp.ones_like(order)
     ocol_ref[...] = as_column(order)
     pcol_ref[...] = as_column(p_order[...])
-    a = sweep(uo_ref[...], ocol_ref[...], uo_ref, order, (always, always), True, None)
+    a = sweep(uo_ref[...], ocol_ref[...], uo_ref, order, (always, always))
     b = sweep(
-        up_ref[...], pcol_ref[...], uo_ref, order,
-        (flag_ref[4:5, :], flag_ref[5:6, :]), True, None,
+        up_ref[...], pcol_ref[...], uo_ref, order, (flag_ref[8:9, :], flag_ref[9:10, :])
     )
     for k in range(2):
         own_ref[k : k + 1, :] = jnp.maximum(a[k], b[k])
@@ -140,56 +142,87 @@
     return lines
 
 
+def put(ref, acc_ref, flag_ref, flag, base=None):
+    for k, line in enumerate(settle(acc_ref, flag_ref, flag)):
+        if base is not None:
+            line = jnp.maximum(line, base[k : k + 1, :])
+        ref[k : k + 1, :] = line
+
+
 def diag_kernel(
     r_ref, r_order, uo_ref, up_ref, ocol_ref, pcol_ref, flag_ref, ret_ref, acc_ref, partner_ref,
     pacc_ref,
 ):
-    role = lax.axis_index("blk") % 4
-
-    @pl.when(role == 2)
-    def _():
-        arrive(r_ref, r_order, ((uo_ref, ocol_ref, 0, acc_ref),), flag_ref, ret_ref)
+    blocks, here, role = position()
+    own, other = (uo_ref, ocol_ref, 0, acc_ref), (up_ref, pcol_ref, 2, pacc_ref)
 
     @pl.when(role == 1)
     def _():
-        held = ((uo_ref, ocol_ref, 0, acc_ref), (up_ref, pcol_ref, 2, pacc_ref))
-        arrive(r_ref, r_order, held, flag_ref, ret_ref)
-        for k, line in enumerate(settle(pacc_ref, flag_ref, 2)):
-            partner_ref[k : k + 1, :] = line
+        arrive(r_ref, r_order, (own, other), flag_ref, ret_ref)
+        put(partner_ref, pacc_ref, flag_ref, 2)
+
+    @pl.when((role == 2) & (here != blocks - 2))
+    def _():
+        arrive(r_ref, r_order, (own,), flag_ref, ret_ref)
+
+    @pl.when(here == blocks - 1)
+    def _():
+        arrive(r_ref, r_order, (other,), flag_ref, ret_ref)
+        put(partner_ref, pacc_ref, flag_ref, 2)
 
 
 def near_kernel(
-    r_ref, r_order, uo_ref, up_ref, ocol_ref, pcol_ref, flag_ref, ret_ref, acc_ref
+    r_ref, r_order, uo_ref, up_ref, ocol_ref, pcol_ref, flag_ref, ret_ref, acc_ref, pacc_ref
 ):
-    _, _, _, outer = position()
-
-    @pl.when(outer)
-    def _():
-        held = ((uo_ref, ocol_ref, 0, acc_ref), (up_ref, pcol_ref, 2, None))
-        arrive(r_ref, r_order, held, flag_ref, ret_ref)
+    _, _, role = position()
+    own, other = (uo_ref, ocol_ref, 4, acc_ref), (up_ref, pcol_ref, 6, pacc_ref)
+
+    @pl.when(role == 0)
+    def _():
+        arrive(r_ref, r_order, (own,), flag_ref, ret_ref)
+
+    @pl.when(role == 3)
+    def _():
+        arrive(r_ref, r_order, (own, other), flag_ref, ret_ref)
+
+
+def partner_last_kernel(partner_ref, near_pacc, flag_ref, out_ref):
+    blocks, here, role = position()
+
+    @pl.when(here == blocks - 1)
+    def _():
+        put(out_ref, near_pacc, flag_ref, 6, partner_ref)
+
+    @pl.when((role == 3) & (here != blocks - 1))
+    def _():
+        put(out_ref, near_pacc, flag_ref, 6)
+
+    @pl.when(role != 3)
+    def _():
+        out_ref[...] = partner_ref[...]
 
 
 def own_last_kernel(own_ref, near_acc, diag_acc, flag_ref, new_ref):
-    _, _, _, outer = position()
-
-    def put(acc_ref):
-        for k, line in enumerate(settle(acc_ref, flag_ref, 0)):
-            new_ref[k : k + 1, :] = jnp.maximum(own_ref[k : k + 1, :], line)
-
-    @pl.when(outer)
-    def _():
-        put(near_acc)
-
-    @pl.when(jnp.logical_not(outer))
-    def _():
-        put(diag_acc)
+    blocks, here, role = position()
+
+    @pl.when((role == 0) | (role == 3))
+    def _():
+        put(new_ref, near_acc, flag_ref, 4, own_ref)
+
+    @pl.when(((role == 1) | (role == 2)) & (here != blocks - 2))
+    def _():
+        put(new_ref, diag_acc, flag_ref, 0, own_ref)
+
+    @pl.when(here == blocks - 2)
+    def _():
+        new_ref[...] = own_ref[...]
 
 
 def last_kernel(own_ref, diag_ref, near_ref, partner_ref, early_ref, late_ref):
-    role = lax.axis_index("blk") % 4
-    _, _, _, outer = position()
-    best = jnp.maximum(own_ref[...], jnp.where(outer, diag_ref[...], near_ref[...]))
-    best = jnp.maximum(best, jnp.where(role == 0, partner_ref[...], FLOOR))
+    _, here, role = position()
+    inner = (role == 1) | (role == 2)
+    best = jnp.maximum(own_ref[...], jnp.where(inner, near_ref[...], diag_ref[...]))
+    best = jnp.maximum(best, jnp.where(here % 2 == 0, partner_ref[...], FLOOR))
     early_ref[...] = best[0]
     late_ref[...] = best[1].astype(late_ref.dtype)
 
@@ -213,20 +246,23 @@
     rows, width = embeddings.shape
     blocks = lax.axis_size("blk")
     order = doc_order.reshape(1, rows)
-    inner = [(i, i ^ 1) for i in range(blocks)]
-    cross = [(i, (i + 2 if i % 2 else i - 2) % blocks) for i in range(blocks)]
-    near = [cross[i] if i % 4 in (1, 2) else inner[i] for i in range(blocks)]
-    diag = [cross[i] if i % 4 in (0, 3) else inner[i] for i in range(blocks)]
+    inner, near, diag = tables(blocks)
 
     def send(x, pairs):
-        return lax.ppermute(x, "blk", pairs)
+        groups = lax.axis_size("groups")
+        whole = [
+            (g * blocks + i, ((g + 1) % groups if i == j else g) * blocks + j)
+            for g in range(groups)
+            for i, j in pairs
+        ]
+        return lax.ppermute(x, ("groups", "blk"), whole)
 
     def back(x, pairs):
         return send(x, [(j, i) for i, j in pairs])
 
     pair = ((2, rows), jnp.float32)
     unit = ((rows, width), jnp.bfloat16)
-    flags = ((6, rows), jnp.int32)
+    flags = ((10, rows), jnp.int32)
     work = 2 * rows * rows * width
 
     e_near = send(embeddings, near)
@@ -246,11 +282,12 @@
         (pltpu.VMEM(*acc),),
     )
     ret_diag = back(ret_diag, diag)
+    ret_near, acc_near, pacc_near = call(
+        near_kernel, (pair, acc, acc), (e_near, o_near, uo, up, ocol, pcol, flag), 2 * work
+    )
+    ret_near = back(ret_near, near)
+    (partner,) = call(partner_last_kernel, (pair,), (partner, pacc_near, flag), work)
     partner = send(partner, inner)
-    ret_near, acc_near = call(
-        near_kernel, (pair, acc), (e_near, o_near, uo, up, ocol, pcol, flag), 2 * work
-    )
-    ret_near = back(ret_near, near)
     (own,) = call(own_last_kernel, (pair,), (own, acc_near, acc_diag, flag), work)
     return call(
         last_kernel, (((rows,), jnp.float32), ((rows,), jnp.bfloat16)),

time: 28.7 us -> 28.3 us (0.986)
  waiting for transfers between devices: 12 us -> 11.5 us
  starting transfers between devices: 9.74 us -> 10.2 us
  Pallas kernels: 4.18 us -> 3.79 us
    ppermute x9, waiting for transfers between devices: 12 us -> 11.5 us  [send(): return lax.ppermute(x, ('groups', 'blk'), whole)]
    ppermute x9, starting transfers between devices: 9.74 us -> 10.2 us  [send(): return lax.ppermute(x, ('groups', 'blk'), whole)]
    pallas_call x5 -> x6, Pallas kernels: 4.18 us -> 3.79 us  [call(): pl.pallas_call(kernel, out_shape=tuple((jax.ShapeDtypeStruct(s, d) for s,...]
  transfers between devices with their start and end apart: 9 -> 9, of which waited for: 3 -> 3; matrix products, arithmetic and copies ran while one was open for 3% -> 3% of each run, Pallas kernels for 13% -> 11%
where the time goes in v6:
time: 28.3 us; the launch traced here: 28.1 us
  waiting for transfers between devices  11.5 us (41%)
  starting transfers between devices  10.2 us (36%)
  Pallas kernels  3.79 us (13%)
  local copies, waits for them, and re-layouts  1.89 us (7%)
  between operations  0.71 us (3%)
    ppermute x9, waiting for transfers between devices, send(): return lax.ppermute(x, ('groups', 'blk'), whole)  11.5 us
    ppermute x9, starting transfers between devices, send(): return lax.ppermute(x, ('groups', 'blk'), whole)  10.2 us
    pallas_call x6, Pallas kernels, call(): pl.pallas_call(kernel, out_shape=tuple((jax.ShapeDtypeStruct(s, d) for s,...  3.79 us
    unnamed x5, local copies, waits for them, and re-layouts  1.89 us
  transfers between devices with their start and end apart: 9, of which 3 were waited for; matrix products, arithmetic and copies ran while one was open for 3% of the time, Pallas kernels for 11%

profile of v6, /device:TPU:0, one launch (start us, length us, event | category | flops | bytes accessed | tf_op | source)
XLA Modules:
  0.0 28.1 jit_solution(3923168248952700713)
XLA Ops:
  0.6 0.6 %collective-permute-start = (bf16[512,768]{1,0:T(8,128)(2,1)}, bf16[512,768]{1,0:T(8,128)(2,1)S(1)}, u32[]{:S(2)}, u32[]{:S(2)}) collective-permute-start(bf16[512,768]{1,0:T(8,128)(2,1)} %e_ref.1), channel_id=1, source_target_pairs={{0,1},{1,0},{2,3},{3,2},{4,5},{5,4},{6,7},{7,6},{8,9},{9,8},{10,11... | collective-permute-start | bytes 2359304 | tf_op jit(solution)/shard_map/ppermute | solution.py:258
  1.2 5.7 %collective-permute-start.4 = (bf16[512,768]{1,0:T(8,128)(2,1)}, bf16[512,768]{1,0:T(8,128)(2,1)S(1)}, u32[]{:S(2)}, u32[]{:S(2)}) collective-permute-start(bf16[512,768]{1,0:T(8,128)(2,1)} %e_ref.1), channel_id=1, source_target_pairs={{0,15},{1,0},{2,3},{3,5},{4,2},{5,4},{6,7},{7,9},{8,6},{9,8},{10,1... | collective-permute-start | bytes 2359304 | tf_op jit(solution)/shard_map/ppermute | solution.py:258
  6.8 0.0 collective-permute-start.2
  6.8 0.0 collective-permute-start.1
  6.9 2.0 %collective-permute-start.5 = (s32[1,512]{1,0:T(1,128)}, s32[1,512]{1,0:T(1,128)S(1)}, u32[]{:S(2)}, u32[]{:S(2)}) collective-permute-start(s32[1,512]{1,0:T(1,128)} %bitcast.2), channel_id=1, source_target_pairs={{0,15},{1,0},{2,3},{3,5},{4,2},{5,4},{6,7},{7,9},{8,6},{9,8},{10,1... | collective-permute-start | bytes 6152 | tf_op jit(solution)/shard_map/ppermute | solution.py:258
  8.8 0.8 %copy.5.lists = s32[16,4]{1,0:T(8,128)S(1)} copy(s32[16,4]{0,1:T(4,128)} %param.5) | data formatting | bytes 512 | tf_op args[2]
  9.6 0.0 collective-permute-done.1.p_order
  9.6 0.0 collective-permute-start.3
  9.6 0.0 collective-permute-done.p_ref
  9.6 0.0 copy-start
  9.6 1.1 %copy-done = bf16[512,768]{1,0:T(8,128)(2,1)S(1)} copy-done((bf16[512,768]{1,0:T(8,128)(2,1)S(1)}, bf16[512,768]{1,0:T(8,128)(2,1)}, u32[]{:S(2)}) %copy-start) | copy-done | bytes 786456
  10.8 2.1 %shard_map.50 = (bf16[512,768]{1,0:T(8,128)(2,1)S(1)}, bf16[512,768]{1,0:T(8,128)(2,1)S(1)}, f32[2,512]{1,0:T(2,128)S(1)}, s32[10,512]{1,0:T(8,128)S(1)}, s32[51...) custom-call(s32[16,4]{1,0:T(8,128)S(1)} %copy.5.lists, bf16[512,768]{1,0:T(8,128)(2,1)S(1)} %copy-done, ...), custom_call_target="tpu_custom_call" | custom-call | flops 805306368 | bytes 3145728 | tf_op jit(solution)/shard_map/pallas_call | solution.py:234
  12.8 3.8 %collective-permute-done.5.r_order = s32[1,512]{1,0:T(1,128)S(1)} collective-permute-done((s32[1,512]{1,0:T(1,128)}, s32[1,512]{1,0:T(1,128)S(1)}, u32[]{:S(2)}, u32[]{:S(2)}) %collective-permute-start.5) | collective-permute-done | bytes 2080 | tf_op jit(solution)/shard_map/ppermute | solution.py:258
  16.7 0.0 collective-permute-done.4.r_ref
  16.7 1.5 %collective-permute-start.6 = (f32[2,512]{1,0:T(2,128)S(1)}, f32[2,512]{1,0:T(2,128)S(1)}, u32[]{:S(2)}, u32[]{:S(2)}) collective-permute-start(f32[2,512]{1,0:T(2,128)S(1)} %get-tuple-element.22), channel_id=1, source_target_pairs={{15,0},{0,1},{3,2},{5,3},{2,4},{4,5},{7,6},{9,7},{6,8},{8,9},{11,1... | collective-permute-start | bytes 12296 | tf_op jit(solution)/shard_map/ppermute | solution.py:258
  18.2 7.1 %collective-permute-done.3.r_order = s32[1,512]{1,0:T(1,128)S(1)} collective-permute-done((s32[1,512]{1,0:T(1,128)S(1)}, s32[1,512]{1,0:T(1,128)S(1)}, u32[]{:S(2)}, u32[]{:S(2)}) %collective-permute-start.3) | collective-permute-done | bytes 2080 | tf_op jit(solution)/shard_map/ppermute | solution.py:258
  25.2 0.0 collective-permute-done.2.r_ref
  25.2 0.9 %shard_map.51 = (f32[2,512]{1,0:T(2,128)S(1)}, f32[1024,128]{1,0:T(8,128)S(1)}, f32[1024,128]{1,0:T(8,128)S(1)}) custom-call(bf16[512,768]{1,0:T(8,128)(2,1)S(1)} %collective-permute-done.2.r_ref, s32[1,512]{1,0:T(1,128)S(1)} %collective-permute-done.3.r_order, bf16[512,768]{1,0:T(8,128)(2,1)S(1)} %get-tuple-element.15.uo_ref, ...), custom_call_target="tpu_custom_call" | custom-call | flops 805306368 | bytes 3145728 | tf_op jit(solution)/shard_map/pallas_call | solution.py:234
  26.1 0.0 collective-permute-start.7
  26.2 0.5 %collective-permute-start.8 = (f32[2,512]{1,0:T(2,128)S(1)}, f32[2,512]{1,0:T(2,128)S(1)}, u32[]{:S(2)}, u32[]{:S(2)}) collective-permute-start(f32[2,512]{1,0:T(2,128)S(1)} %shard_map.54), channel_id=1, source_target_pairs={{0,1},{1,0},{2,3},{3,2},{4,5},{5,4},{6,7},{7,6},{8,9},{9,8},{10,11... | collective-permute-start | bytes 12296 | tf_op jit(solution)/shard_map/ppermute | solution.py:258
  26.7 0.2 shard_map.53.own_ref
  26.9 0.0 collective-permute-done.6.diag_ref
  26.9 0.6 %collective-permute-done.7.near_ref = f32[2,512]{1,0:T(2,128)S(1)} collective-permute-done((f32[2,512]{1,0:T(2,128)S(1)}, f32[2,512]{1,0:T(2,128)S(1)}, u32[]{:S(2)}, u32[]{:S(2)}) %collective-permute-start.7) | collective-permute-done | bytes 4128 | tf_op jit(solution)/shard_map/ppermute | solution.py:258
  27.5 0.6 %shard_map.55 = (f32[512]{0:T(512)}, bf16[512]{0:T(512)(128)(2,1)}) custom-call(f32[2,512]{1,0:T(2,128)S(1)} %shard_map.53.own_ref, f32[2,512]{1,0:T(2,128)S(1)} %collective-permute-done.6.diag_ref, f32[2,512]{1,0:T(2,128)S(1)} %collective-permute-done.7.near_ref, f32[2,512]{1,0:T(2,128)S(1)} %collective-permute-done.8.partner_ref), custom_call_target="tpu_custom_call" | custom-call | bytes 3145728 | tf_op jit(solution)/shard_map/pallas_call | solution.py:234
  (5 shorter events, 0.0 us)
Async XLA Ops:
  0.6 9.0 %collective-permute-start = (bf16[512,768]{1,0:T(8,128)(2,1)}, bf16[512,768]{1,0:T(8,128)(2,1)S(1)}, u32[]{:S(2)}, u32[]{:S(2)}) collective-permute-start(bf16[512,768]{1,0:T(8,128)(2,1)} %e_ref.1), channel_id=1, source_target_pairs={{0,1},{1,0},{2,3},{3,2},{4,5},{5,4},{6,7},{7,6},{8,9},{9,8},{10,11... | collective-permute-start | bytes 2359304 | tf_op jit(solution)/shard_map/ppermute | solution.py:258
  1.2 15.5 %collective-permute-start.4 = (bf16[512,768]{1,0:T(8,128)(2,1)}, bf16[512,768]{1,0:T(8,128)(2,1)S(1)}, u32[]{:S(2)}, u32[]{:S(2)}) collective-permute-start(bf16[512,768]{1,0:T(8,128)(2,1)} %e_ref.1), channel_id=1, source_target_pairs={{0,15},{1,0},{2,3},{3,5},{4,2},{5,4},{6,7},{7,9},{8,6},{9,8},{10,1... | collective-permute-start | bytes 2359304 | tf_op jit(solution)/shard_map/ppermute | solution.py:258
  6.8 18.4 %collective-permute-start.2 = (bf16[512,768]{1,0:T(8,128)(2,1)}, bf16[512,768]{1,0:T(8,128)(2,1)S(1)}, u32[]{:S(2)}, u32[]{:S(2)}) collective-permute-start(bf16[512,768]{1,0:T(8,128)(2,1)} %e_ref.1), channel_id=1, source_target_pairs={{0,1},{1,3},{2,0},{3,2},{4,5},{5,7},{6,4},{7,6},{8,9},{9,11},{10,8... | collective-permute-start | bytes 2359304 | tf_op jit(solution)/shard_map/ppermute | solution.py:258
  6.8 2.8 %copy-start.1 = (s32[512]{0:T(512)S(1)}, s32[512]{0:T(512)}, u32[]{:S(2)}) copy-start(s32[512]{0:T(512)} %param.4) | copy-start | bytes 6148
  6.8 2.7 %collective-permute-start.1 = (s32[1,512]{1,0:T(1,128)}, s32[1,512]{1,0:T(1,128)S(1)}, u32[]{:S(2)}, u32[]{:S(2)}) collective-permute-start(s32[1,512]{1,0:T(1,128)} %bitcast.1), channel_id=1, source_target_pairs={{0,1},{1,0},{2,3},{3,2},{4,5},{5,4},{6,7},{7,6},{8,9},{9,8},{10,11... | collective-permute-start | bytes 6152 | tf_op jit(solution)/shard_map/ppermute | solution.py:258
  6.9 9.8 %collective-permute-start.5 = (s32[1,512]{1,0:T(1,128)}, s32[1,512]{1,0:T(1,128)S(1)}, u32[]{:S(2)}, u32[]{:S(2)}) collective-permute-start(s32[1,512]{1,0:T(1,128)} %bitcast.2), channel_id=1, source_target_pairs={{0,15},{1,0},{2,3},{3,5},{4,2},{5,4},{6,7},{7,9},{8,6},{9,8},{10,1... | collective-permute-start | bytes 6152 | tf_op jit(solution)/shard_map/ppermute | solution.py:258
  9.6 15.6 %collective-permute-start.3 = (s32[1,512]{1,0:T(1,128)S(1)}, s32[1,512]{1,0:T(1,128)S(1)}, u32[]{:S(2)}, u32[]{:S(2)}) collective-permute-start(s32[1,512]{1,0:T(1,128)S(1)} %bitcast.3), channel_id=1, source_target_pairs={{0,1},{1,3},{2,0},{3,2},{4,5},{5,7},{6,4},{7,6},{8,9},{9,11},{10,8... | collective-permute-start | bytes 6152 | tf_op jit(solution)/shard_map/ppermute | solution.py:258
  9.6 1.1 %copy-start = (bf16[512,768]{1,0:T(8,128)(2,1)S(1)}, bf16[512,768]{1,0:T(8,128)(2,1)}, u32[]{:S(2)}) copy-start(bf16[512,768]{1,0:T(8,128)(2,1)} %e_ref.1) | copy-start | bytes 2359300
  16.7 10.2 %collective-permute-start.6 = (f32[2,512]{1,0:T(2,128)S(1)}, f32[2,512]{1,0:T(2,128)S(1)}, u32[]{:S(2)}, u32[]{:S(2)}) collective-permute-start(f32[2,512]{1,0:T(2,128)S(1)} %get-tuple-element.22), channel_id=1, source_target_pairs={{15,0},{0,1},{3,2},{5,3},{2,4},{4,5},{7,6},{9,7},{6,8},{8,9},{11,1... | collective-permute-start | bytes 12296 | tf_op jit(solution)/shard_map/ppermute | solution.py:258
  26.1 1.4 %collective-permute-start.7 = (f32[2,512]{1,0:T(2,128)S(1)}, f32[2,512]{1,0:T(2,128)S(1)}, u32[]{:S(2)}, u32[]{:S(2)}) collective-permute-start(f32[2,512]{1,0:T(2,128)S(1)} %get-tuple-element.23), channel_id=1, source_target_pairs={{1,0},{3,1},{0,2},{2,3},{5,4},{7,5},{4,6},{6,7},{9,8},{11,9},{8,10... | collective-permute-start | bytes 12296 | tf_op jit(solution)/shard_map/ppermute | solution.py:258
  26.2 1.3 %collective-permute-start.8 = (f32[2,512]{1,0:T(2,128)S(1)}, f32[2,512]{1,0:T(2,128)S(1)}, u32[]{:S(2)}, u32[]{:S(2)}) collective-permute-start(f32[2,512]{1,0:T(2,128)S(1)} %shard_map.54), channel_id=1, source_target_pairs={{0,1},{1,0},{2,3},{3,2},{4,5},{5,4},{6,7},{7,6},{8,9},{9,8},{10,11... | collective-permute-start | bytes 12296 | tf_op jit(solution)/shard_map/ppermute | solution.py:258

commit v7 on v6

--- a/solution.py
+++ b/solution.py
@@ -98,13 +98,18 @@
 
 
 def arrive(r_ref, r_order, held, flag_ref, ret_ref):
-    units = normalize(r_ref[...])
+    raw = r_ref[...]
     order = r_order[...]
-    rows = r_ref.shape[0]
+    rows, width = r_ref.shape
+    squares = None
+    for at in range(0, width, LANES):
+        values = raw[:, at : at + LANES].astype(jnp.float32)
+        squares = values * values if squares is None else squares + values * values
+    inverse = lax.rsqrt(jnp.sum(squares.T, axis=0, keepdims=True) + 1e-06)
     best = [None, None]
     for held_ref, col_ref, flag, acc_ref in held:
         scores = lax.dot_general(
-            held_ref[...], units, (((1,), (1,)), ((), ())), preferred_element_type=jnp.float32
+            held_ref[...], raw, (((1,), (1,)), ((), ())), preferred_element_type=jnp.float32
         )
         run = [[None] * (rows // LANES) for _ in range(2)]
         for at in range(0, rows, STRIP):
@@ -112,7 +117,8 @@
             wide = [None, None]
             for tile in range(rows // LANES):
                 span = slice(tile * LANES, tile * LANES + LANES)
-                piece = scores[at : at + STRIP, span]
+                scale = inverse[:, span]
+                piece = jnp.where(scale > 0, scores[at : at + STRIP, span] * scale, 0.0)
                 after = order[:, span] > col
                 parts = (jnp.where(after, piece, FLOOR), jnp.where(after, FLOOR, piece))
                 for k in range(2):

time: 28.3 us -> 28.2 us (level)
  no operation moved by 1% of the time
where the time goes in v7:
time: 28.2 us; the launch traced here: 28 us
  waiting for transfers between devices  11.5 us (41%)
  starting transfers between devices  10.2 us (36%)
  Pallas kernels  3.71 us (13%)
  local copies, waits for them, and re-layouts  1.89 us (7%)
  between operations  0.71 us (3%)
    ppermute x9, waiting for transfers between devices, send(): return lax.ppermute(x, ('groups', 'blk'), whole)  11.5 us
    ppermute x9, starting transfers between devices, send(): return lax.ppermute(x, ('groups', 'blk'), whole)  10.2 us
    pallas_call x6, Pallas kernels, call(): pl.pallas_call(kernel, out_shape=tuple((jax.ShapeDtypeStruct(s, d) for s,...  3.71 us
    unnamed x5, local copies, waits for them, and re-layouts  1.89 us
  transfers between devices with their start and end apart: 9, of which 3 were waited for; matrix products, arithmetic and copies ran while one was open for 3% of the time, Pallas kernels for 11%

profile of v7, /device:TPU:0, one launch (start us, length us, event | category | flops | bytes accessed | tf_op | source)
XLA Modules:
  0.0 28.0 jit_solution(5931374702469726121)
XLA Ops:
  0.6 0.6 %collective-permute-start = (bf16[512,768]{1,0:T(8,128)(2,1)}, bf16[512,768]{1,0:T(8,128)(2,1)S(1)}, u32[]{:S(2)}, u32[]{:S(2)}) collective-permute-start(bf16[512,768]{1,0:T(8,128)(2,1)} %e_ref.1), channel_id=1, source_target_pairs={{0,1},{1,0},{2,3},{3,2},{4,5},{5,4},{6,7},{7,6},{8,9},{9,8},{10,11... | collective-permute-start | bytes 2359304 | tf_op jit(solution)/shard_map/ppermute | solution.py:264
  1.2 5.7 %collective-permute-start.4 = (bf16[512,768]{1,0:T(8,128)(2,1)}, bf16[512,768]{1,0:T(8,128)(2,1)S(1)}, u32[]{:S(2)}, u32[]{:S(2)}) collective-permute-start(bf16[512,768]{1,0:T(8,128)(2,1)} %e_ref.1), channel_id=1, source_target_pairs={{0,15},{1,0},{2,3},{3,5},{4,2},{5,4},{6,7},{7,9},{8,6},{9,8},{10,1... | collective-permute-start | bytes 2359304 | tf_op jit(solution)/shard_map/ppermute | solution.py:264
  6.8 0.0 collective-permute-start.2
  6.8 0.0 collective-permute-start.1
  6.9 2.0 %collective-permute-start.5 = (s32[1,512]{1,0:T(1,128)}, s32[1,512]{1,0:T(1,128)S(1)}, u32[]{:S(2)}, u32[]{:S(2)}) collective-permute-start(s32[1,512]{1,0:T(1,128)} %bitcast.2), channel_id=1, source_target_pairs={{0,15},{1,0},{2,3},{3,5},{4,2},{5,4},{6,7},{7,9},{8,6},{9,8},{10,1... | collective-permute-start | bytes 6152 | tf_op jit(solution)/shard_map/ppermute | solution.py:264
  8.8 0.8 %copy.5.lists = s32[16,4]{1,0:T(8,128)S(1)} copy(s32[16,4]{0,1:T(4,128)} %param.5) | data formatting | bytes 512 | tf_op args[2]
  9.6 0.0 collective-permute-done.1.p_order
  9.6 0.0 collective-permute-start.3
  9.6 0.0 collective-permute-done.p_ref
  9.6 0.0 copy-start
  9.6 1.1 %copy-done = bf16[512,768]{1,0:T(8,128)(2,1)S(1)} copy-done((bf16[512,768]{1,0:T(8,128)(2,1)S(1)}, bf16[512,768]{1,0:T(8,128)(2,1)}, u32[]{:S(2)}) %copy-start) | copy-done | bytes 786456
  10.8 2.1 %shard_map.50 = (bf16[512,768]{1,0:T(8,128)(2,1)S(1)}, bf16[512,768]{1,0:T(8,128)(2,1)S(1)}, f32[2,512]{1,0:T(2,128)S(1)}, s32[10,512]{1,0:T(8,128)S(1)}, s32[51...) custom-call(s32[16,4]{1,0:T(8,128)S(1)} %copy.5.lists, bf16[512,768]{1,0:T(8,128)(2,1)S(1)} %copy-done, ...), custom_call_target="tpu_custom_call" | custom-call | flops 805306368 | bytes 3145728 | tf_op jit(solution)/shard_map/pallas_call | solution.py:240
  12.8 3.8 %collective-permute-done.5.r_order = s32[1,512]{1,0:T(1,128)S(1)} collective-permute-done((s32[1,512]{1,0:T(1,128)}, s32[1,512]{1,0:T(1,128)S(1)}, u32[]{:S(2)}, u32[]{:S(2)}) %collective-permute-start.5) | collective-permute-done | bytes 2080 | tf_op jit(solution)/shard_map/ppermute | solution.py:264
  16.7 0.0 collective-permute-done.4.r_ref
  16.7 1.5 %collective-permute-start.6 = (f32[2,512]{1,0:T(2,128)S(1)}, f32[2,512]{1,0:T(2,128)S(1)}, u32[]{:S(2)}, u32[]{:S(2)}) collective-permute-start(f32[2,512]{1,0:T(2,128)S(1)} %get-tuple-element.22), channel_id=1, source_target_pairs={{15,0},{0,1},{3,2},{5,3},{2,4},{4,5},{7,6},{9,7},{6,8},{8,9},{11,1... | collective-permute-start | bytes 12296 | tf_op jit(solution)/shard_map/ppermute | solution.py:264
  18.2 7.1 %collective-permute-done.3.r_order = s32[1,512]{1,0:T(1,128)S(1)} collective-permute-done((s32[1,512]{1,0:T(1,128)S(1)}, s32[1,512]{1,0:T(1,128)S(1)}, u32[]{:S(2)}, u32[]{:S(2)}) %collective-permute-start.3) | collective-permute-done | bytes 2080 | tf_op jit(solution)/shard_map/ppermute | solution.py:264
  25.2 0.0 collective-permute-done.2.r_ref
  25.2 0.8 %shard_map.51 = (f32[2,512]{1,0:T(2,128)S(1)}, f32[1024,128]{1,0:T(8,128)S(1)}, f32[1024,128]{1,0:T(8,128)S(1)}) custom-call(bf16[512,768]{1,0:T(8,128)(2,1)S(1)} %collective-permute-done.2.r_ref, s32[1,512]{1,0:T(1,128)S(1)} %collective-permute-done.3.r_order, bf16[512,768]{1,0:T(8,128)(2,1)S(1)} %get-tuple-element.15.uo_ref, ...), custom_call_target="tpu_custom_call" | custom-call | flops 805306368 | bytes 3145728 | tf_op jit(solution)/shard_map/pallas_call | solution.py:240
  26.0 0.0 collective-permute-start.7
  26.1 0.5 %collective-permute-start.8 = (f32[2,512]{1,0:T(2,128)S(1)}, f32[2,512]{1,0:T(2,128)S(1)}, u32[]{:S(2)}, u32[]{:S(2)}) collective-permute-start(f32[2,512]{1,0:T(2,128)S(1)} %shard_map.54), channel_id=1, source_target_pairs={{0,1},{1,0},{2,3},{3,2},{4,5},{5,4},{6,7},{7,6},{8,9},{9,8},{10,11... | collective-permute-start | bytes 12296 | tf_op jit(solution)/shard_map/ppermute | solution.py:264
  26.6 0.2 shard_map.53.own_ref
  26.8 0.0 collective-permute-done.6.diag_ref
  26.8 0.6 %collective-permute-done.7.near_ref = f32[2,512]{1,0:T(2,128)S(1)} collective-permute-done((f32[2,512]{1,0:T(2,128)S(1)}, f32[2,512]{1,0:T(2,128)S(1)}, u32[]{:S(2)}, u32[]{:S(2)}) %collective-permute-start.7) | collective-permute-done | bytes 4128 | tf_op jit(solution)/shard_map/ppermute | solution.py:264
  27.4 0.6 %shard_map.55 = (f32[512]{0:T(512)}, bf16[512]{0:T(512)(128)(2,1)}) custom-call(f32[2,512]{1,0:T(2,128)S(1)} %shard_map.53.own_ref, f32[2,512]{1,0:T(2,128)S(1)} %collective-permute-done.6.diag_ref, f32[2,512]{1,0:T(2,128)S(1)} %collective-permute-done.7.near_ref, f32[2,512]{1,0:T(2,128)S(1)} %collective-permute-done.8.partner_ref), custom_call_target="tpu_custom_call" | custom-call | bytes 3145728 | tf_op jit(solution)/shard_map/pallas_call | solution.py:240
  (5 shorter events, 0.0 us)
Async XLA Ops:
  0.6 9.0 %collective-permute-start = (bf16[512,768]{1,0:T(8,128)(2,1)}, bf16[512,768]{1,0:T(8,128)(2,1)S(1)}, u32[]{:S(2)}, u32[]{:S(2)}) collective-permute-start(bf16[512,768]{1,0:T(8,128)(2,1)} %e_ref.1), channel_id=1, source_target_pairs={{0,1},{1,0},{2,3},{3,2},{4,5},{5,4},{6,7},{7,6},{8,9},{9,8},{10,11... | collective-permute-start | bytes 2359304 | tf_op jit(solution)/shard_map/ppermute | solution.py:264
  1.2 15.5 %collective-permute-start.4 = (bf16[512,768]{1,0:T(8,128)(2,1)}, bf16[512,768]{1,0:T(8,128)(2,1)S(1)}, u32[]{:S(2)}, u32[]{:S(2)}) collective-permute-start(bf16[512,768]{1,0:T(8,128)(2,1)} %e_ref.1), channel_id=1, source_target_pairs={{0,15},{1,0},{2,3},{3,5},{4,2},{5,4},{6,7},{7,9},{8,6},{9,8},{10,1... | collective-permute-start | bytes 2359304 | tf_op jit(solution)/shard_map/ppermute | solution.py:264
  6.8 18.4 %collective-permute-start.2 = (bf16[512,768]{1,0:T(8,128)(2,1)}, bf16[512,768]{1,0:T(8,128)(2,1)S(1)}, u32[]{:S(2)}, u32[]{:S(2)}) collective-permute-start(bf16[512,768]{1,0:T(8,128)(2,1)} %e_ref.1), channel_id=1, source_target_pairs={{0,1},{1,3},{2,0},{3,2},{4,5},{5,7},{6,4},{7,6},{8,9},{9,11},{10,8... | collective-permute-start | bytes 2359304 | tf_op jit(solution)/shard_map/ppermute | solution.py:264
  6.8 2.8 %copy-start.1 = (s32[512]{0:T(512)S(1)}, s32[512]{0:T(512)}, u32[]{:S(2)}) copy-start(s32[512]{0:T(512)} %param.4) | copy-start | bytes 6148
  6.8 2.7 %collective-permute-start.1 = (s32[1,512]{1,0:T(1,128)}, s32[1,512]{1,0:T(1,128)S(1)}, u32[]{:S(2)}, u32[]{:S(2)}) collective-permute-start(s32[1,512]{1,0:T(1,128)} %bitcast.1), channel_id=1, source_target_pairs={{0,1},{1,0},{2,3},{3,2},{4,5},{5,4},{6,7},{7,6},{8,9},{9,8},{10,11... | collective-permute-start | bytes 6152 | tf_op jit(solution)/shard_map/ppermute | solution.py:264
  6.9 9.8 %collective-permute-start.5 = (s32[1,512]{1,0:T(1,128)}, s32[1,512]{1,0:T(1,128)S(1)}, u32[]{:S(2)}, u32[]{:S(2)}) collective-permute-start(s32[1,512]{1,0:T(1,128)} %bitcast.2), channel_id=1, source_target_pairs={{0,15},{1,0},{2,3},{3,5},{4,2},{5,4},{6,7},{7,9},{8,6},{9,8},{10,1... | collective-permute-start | bytes 6152 | tf_op jit(solution)/shard_map/ppermute | solution.py:264
  9.6 15.6 %collective-permute-start.3 = (s32[1,512]{1,0:T(1,128)S(1)}, s32[1,512]{1,0:T(1,128)S(1)}, u32[]{:S(2)}, u32[]{:S(2)}) collective-permute-start(s32[1,512]{1,0:T(1,128)S(1)} %bitcast.3), channel_id=1, source_target_pairs={{0,1},{1,3},{2,0},{3,2},{4,5},{5,7},{6,4},{7,6},{8,9},{9,11},{10,8... | collective-permute-start | bytes 6152 | tf_op jit(solution)/shard_map/ppermute | solution.py:264
  9.6 1.1 %copy-start = (bf16[512,768]{1,0:T(8,128)(2,1)S(1)}, bf16[512,768]{1,0:T(8,128)(2,1)}, u32[]{:S(2)}) copy-start(bf16[512,768]{1,0:T(8,128)(2,1)} %e_ref.1) | copy-start | bytes 2359300
  16.7 10.1 %collective-permute-start.6 = (f32[2,512]{1,0:T(2,128)S(1)}, f32[2,512]{1,0:T(2,128)S(1)}, u32[]{:S(2)}, u32[]{:S(2)}) collective-permute-start(f32[2,512]{1,0:T(2,128)S(1)} %get-tuple-element.22), channel_id=1, source_target_pairs={{15,0},{0,1},{3,2},{5,3},{2,4},{4,5},{7,6},{9,7},{6,8},{8,9},{11,1... | collective-permute-start | bytes 12296 | tf_op jit(solution)/shard_map/ppermute | solution.py:264
  26.0 1.4 %collective-permute-start.7 = (f32[2,512]{1,0:T(2,128)S(1)}, f32[2,512]{1,0:T(2,128)S(1)}, u32[]{:S(2)}, u32[]{:S(2)}) collective-permute-start(f32[2,512]{1,0:T(2,128)S(1)} %get-tuple-element.23), channel_id=1, source_target_pairs={{1,0},{3,1},{0,2},{2,3},{5,4},{7,5},{4,6},{6,7},{9,8},{11,9},{8,10... | collective-permute-start | bytes 12296 | tf_op jit(solution)/shard_map/ppermute | solution.py:264
  26.1 1.3 %collective-permute-start.8 = (f32[2,512]{1,0:T(2,128)S(1)}, f32[2,512]{1,0:T(2,128)S(1)}, u32[]{:S(2)}, u32[]{:S(2)}) collective-permute-start(f32[2,512]{1,0:T(2,128)S(1)} %shard_map.54), channel_id=1, source_target_pairs={{0,1},{1,0},{2,3},{3,2},{4,5},{5,4},{6,7},{7,6},{8,9},{9,8},{10,11... | collective-permute-start | bytes 12296 | tf_op jit(solution)/shard_map/ppermute | solution.py:264

commit v8 on v7

--- a/solution.py
+++ b/solution.py
@@ -7,7 +7,7 @@
 
 
 LANES = 128
-STRIP = 32
+STRIP = 64
 FLOOR = -1.0
 
 
@@ -99,8 +99,11 @@
 
 def arrive(r_ref, r_order, held, flag_ref, ret_ref):
     raw = r_ref[...]
+    bound = jnp.asarray(2.0**64, raw.dtype)
+    bounded = jnp.minimum(jnp.maximum(raw, -bound), bound)
     order = r_order[...]
     rows, width = r_ref.shape
+    block = rows // 2
     squares = None
     for at in range(0, width, LANES):
         values = raw[:, at : at + LANES].astype(jnp.float32)
@@ -108,17 +111,19 @@
     inverse = lax.rsqrt(jnp.sum(squares.T, axis=0, keepdims=True) + 1e-06)
     best = [None, None]
     for held_ref, col_ref, flag, acc_ref in held:
-        scores = lax.dot_general(
-            held_ref[...], raw, (((1,), (1,)), ((), ())), preferred_element_type=jnp.float32
-        )
         run = [[None] * (rows // LANES) for _ in range(2)]
         for at in range(0, rows, STRIP):
+            if at % block == 0:
+                scores = lax.dot_general(
+                    held_ref[at : at + block, :], bounded, (((1,), (1,)), ((), ())),
+                    preferred_element_type=jnp.float32,
+                )
+            row = at % block
             col = col_ref[at : at + STRIP, :]
             wide = [None, None]
             for tile in range(rows // LANES):
                 span = slice(tile * LANES, tile * LANES + LANES)
-                scale = inverse[:, span]
-                piece = jnp.where(scale > 0, scores[at : at + STRIP, span] * scale, 0.0)
+                piece = scores[row : row + STRIP, span] * inverse[:, span]
                 after = order[:, span] > col
                 parts = (jnp.where(after, piece, FLOOR), jnp.where(after, FLOOR, piece))
                 for k in range(2):

time: 28.2 us -> 28.1 us (level)
  no operation moved by 1% of the time
where the time goes in v8:
time: 28.1 us; the launch traced here: 27.9 us
  waiting for transfers between devices  11.6 us (41%)
  starting transfers between devices  10.1 us (36%)
  Pallas kernels  3.65 us (13%)
  local copies, waits for them, and re-layouts  1.89 us (7%)
  between operations  0.71 us (3%)
    ppermute x9, waiting for transfers between devices, send(): return lax.ppermute(x, ('groups', 'blk'), whole)  11.6 us
    ppermute x9, starting transfers between devices, send(): return lax.ppermute(x, ('groups', 'blk'), whole)  10.1 us
    pallas_call x6, Pallas kernels, call(): pl.pallas_call(kernel, out_shape=tuple((jax.ShapeDtypeStruct(s, d) for s,...  3.65 us
    unnamed x5, local copies, waits for them, and re-layouts  1.89 us
  transfers between devices with their start and end apart: 9, of which 3 were waited for; matrix products, arithmetic and copies ran while one was open for 3% of the time, Pallas kernels for 11%

profile of v8, /device:TPU:0, one launch (start us, length us, event | category | flops | bytes accessed | tf_op | source)
XLA Modules:
  0.0 27.9 jit_solution(9756693041809964233)
XLA Ops:
  0.6 0.6 %collective-permute-start = (bf16[512,768]{1,0:T(8,128)(2,1)}, bf16[512,768]{1,0:T(8,128)(2,1)S(1)}, u32[]{:S(2)}, u32[]{:S(2)}) collective-permute-start(bf16[512,768]{1,0:T(8,128)(2,1)} %e_ref.1), channel_id=1, source_target_pairs={{0,1},{1,0},{2,3},{3,2},{4,5},{5,4},{6,7},{7,6},{8,9},{9,8},{10,11... | collective-permute-start | bytes 2359304 | tf_op jit(solution)/shard_map/ppermute | solution.py:269
  1.2 5.7 %collective-permute-start.4 = (bf16[512,768]{1,0:T(8,128)(2,1)}, bf16[512,768]{1,0:T(8,128)(2,1)S(1)}, u32[]{:S(2)}, u32[]{:S(2)}) collective-permute-start(bf16[512,768]{1,0:T(8,128)(2,1)} %e_ref.1), channel_id=1, source_target_pairs={{0,15},{1,0},{2,3},{3,5},{4,2},{5,4},{6,7},{7,9},{8,6},{9,8},{10,1... | collective-permute-start | bytes 2359304 | tf_op jit(solution)/shard_map/ppermute | solution.py:269
  6.8 0.0 collective-permute-start.2
  6.8 0.0 collective-permute-start.1
  6.9 2.0 %collective-permute-start.5 = (s32[1,512]{1,0:T(1,128)}, s32[1,512]{1,0:T(1,128)S(1)}, u32[]{:S(2)}, u32[]{:S(2)}) collective-permute-start(s32[1,512]{1,0:T(1,128)} %bitcast.2), channel_id=1, source_target_pairs={{0,15},{1,0},{2,3},{3,5},{4,2},{5,4},{6,7},{7,9},{8,6},{9,8},{10,1... | collective-permute-start | bytes 6152 | tf_op jit(solution)/shard_map/ppermute | solution.py:269
  8.8 0.8 %copy.5.lists = s32[16,4]{1,0:T(8,128)S(1)} copy(s32[16,4]{0,1:T(4,128)} %param.5) | data formatting | bytes 512 | tf_op args[2]
  9.6 0.0 collective-permute-done.1.p_order
  9.6 0.0 collective-permute-start.3
  9.6 0.0 copy-start
  9.6 1.1 %copy-done = bf16[512,768]{1,0:T(8,128)(2,1)S(1)} copy-done((bf16[512,768]{1,0:T(8,128)(2,1)S(1)}, bf16[512,768]{1,0:T(8,128)(2,1)}, u32[]{:S(2)}) %copy-start) | copy-done | bytes 786456
  10.8 2.1 %shard_map.50 = (bf16[512,768]{1,0:T(8,128)(2,1)S(1)}, bf16[512,768]{1,0:T(8,128)(2,1)S(1)}, f32[2,512]{1,0:T(2,128)S(1)}, s32[10,512]{1,0:T(8,128)S(1)}, s32[51...) custom-call(s32[16,4]{1,0:T(8,128)S(1)} %copy.5.lists, bf16[512,768]{1,0:T(8,128)(2,1)S(1)} %copy-done, ...), custom_call_target="tpu_custom_call" | custom-call | flops 805306368 | bytes 3145728 | tf_op jit(solution)/shard_map/pallas_call | solution.py:245
  12.8 3.8 %collective-permute-done.5.r_order = s32[1,512]{1,0:T(1,128)S(1)} collective-permute-done((s32[1,512]{1,0:T(1,128)}, s32[1,512]{1,0:T(1,128)S(1)}, u32[]{:S(2)}, u32[]{:S(2)}) %collective-permute-start.5) | collective-permute-done | bytes 2080 | tf_op jit(solution)/shard_map/ppermute | solution.py:269
  16.7 0.0 collective-permute-done.4.r_ref
  16.7 1.4 %collective-permute-start.6 = (f32[2,512]{1,0:T(2,128)S(1)}, f32[2,512]{1,0:T(2,128)S(1)}, u32[]{:S(2)}, u32[]{:S(2)}) collective-permute-start(f32[2,512]{1,0:T(2,128)S(1)} %get-tuple-element.22), channel_id=1, source_target_pairs={{15,0},{0,1},{3,2},{5,3},{2,4},{4,5},{7,6},{9,7},{6,8},{8,9},{11,1... | collective-permute-start | bytes 12296 | tf_op jit(solution)/shard_map/ppermute | solution.py:269
  18.0 7.2 %collective-permute-done.3.r_order = s32[1,512]{1,0:T(1,128)S(1)} collective-permute-done((s32[1,512]{1,0:T(1,128)S(1)}, s32[1,512]{1,0:T(1,128)S(1)}, u32[]{:S(2)}, u32[]{:S(2)}) %collective-permute-start.3) | collective-permute-done | bytes 2080 | tf_op jit(solution)/shard_map/ppermute | solution.py:269
  25.2 0.0 collective-permute-done.2.r_ref
  25.2 0.7 %shard_map.51 = (f32[2,512]{1,0:T(2,128)S(1)}, f32[1024,128]{1,0:T(8,128)S(1)}, f32[1024,128]{1,0:T(8,128)S(1)}) custom-call(bf16[512,768]{1,0:T(8,128)(2,1)S(1)} %collective-permute-done.2.r_ref, s32[1,512]{1,0:T(1,128)S(1)} %collective-permute-done.3.r_order, bf16[512,768]{1,0:T(8,128)(2,1)S(1)} %get-tuple-element.15.uo_ref, ...), custom_call_target="tpu_custom_call" | custom-call | flops 805306368 | bytes 3145728 | tf_op jit(solution)/shard_map/pallas_call | solution.py:245
  26.0 0.0 collective-permute-start.7
  26.1 0.5 %collective-permute-start.8 = (f32[2,512]{1,0:T(2,128)S(1)}, f32[2,512]{1,0:T(2,128)S(1)}, u32[]{:S(2)}, u32[]{:S(2)}) collective-permute-start(f32[2,512]{1,0:T(2,128)S(1)} %shard_map.54), channel_id=1, source_target_pairs={{0,1},{1,0},{2,3},{3,2},{4,5},{5,4},{6,7},{7,6},{8,9},{9,8},{10,11... | collective-permute-start | bytes 12296 | tf_op jit(solution)/shard_map/ppermute | solution.py:269
  26.5 0.2 shard_map.53.own_ref
  26.7 0.0 collective-permute-done.6.diag_ref
  26.8 0.6 %collective-permute-done.7.near_ref = f32[2,512]{1,0:T(2,128)S(1)} collective-permute-done((f32[2,512]{1,0:T(2,128)S(1)}, f32[2,512]{1,0:T(2,128)S(1)}, u32[]{:S(2)}, u32[]{:S(2)}) %collective-permute-start.7) | collective-permute-done | bytes 4128 | tf_op jit(solution)/shard_map/ppermute | solution.py:269
  27.3 0.0 collective-permute-done.8.partner_ref
  27.3 0.6 %shard_map.55 = (f32[512]{0:T(512)}, bf16[512]{0:T(512)(128)(2,1)}) custom-call(f32[2,512]{1,0:T(2,128)S(1)} %shard_map.53.own_ref, f32[2,512]{1,0:T(2,128)S(1)} %collective-permute-done.6.diag_ref, f32[2,512]{1,0:T(2,128)S(1)} %collective-permute-done.7.near_ref, f32[2,512]{1,0:T(2,128)S(1)} %collective-permute-done.8.partner_ref), custom_call_target="tpu_custom_call" | custom-call | bytes 3145728 | tf_op jit(solution)/shard_map/pallas_call | solution.py:245
  (5 shorter events, 0.0 us)
Async XLA Ops:
  0.6 9.0 %collective-permute-start = (bf16[512,768]{1,0:T(8,128)(2,1)}, bf16[512,768]{1,0:T(8,128)(2,1)S(1)}, u32[]{:S(2)}, u32[]{:S(2)}) collective-permute-start(bf16[512,768]{1,0:T(8,128)(2,1)} %e_ref.1), channel_id=1, source_target_pairs={{0,1},{1,0},{2,3},{3,2},{4,5},{5,4},{6,7},{7,6},{8,9},{9,8},{10,11... | collective-permute-start | bytes 2359304 | tf_op jit(solution)/shard_map/ppermute | solution.py:269
  1.2 15.5 %collective-permute-start.4 = (bf16[512,768]{1,0:T(8,128)(2,1)}, bf16[512,768]{1,0:T(8,128)(2,1)S(1)}, u32[]{:S(2)}, u32[]{:S(2)}) collective-permute-start(bf16[512,768]{1,0:T(8,128)(2,1)} %e_ref.1), channel_id=1, source_target_pairs={{0,15},{1,0},{2,3},{3,5},{4,2},{5,4},{6,7},{7,9},{8,6},{9,8},{10,1... | collective-permute-start | bytes 2359304 | tf_op jit(solution)/shard_map/ppermute | solution.py:269
  6.8 18.4 %collective-permute-start.2 = (bf16[512,768]{1,0:T(8,128)(2,1)}, bf16[512,768]{1,0:T(8,128)(2,1)S(1)}, u32[]{:S(2)}, u32[]{:S(2)}) collective-permute-start(bf16[512,768]{1,0:T(8,128)(2,1)} %e_ref.1), channel_id=1, source_target_pairs={{0,1},{1,3},{2,0},{3,2},{4,5},{5,7},{6,4},{7,6},{8,9},{9,11},{10,8... | collective-permute-start | bytes 2359304 | tf_op jit(solution)/shard_map/ppermute | solution.py:269
  6.8 2.8 %copy-start.1 = (s32[512]{0:T(512)S(1)}, s32[512]{0:T(512)}, u32[]{:S(2)}) copy-start(s32[512]{0:T(512)} %param.4) | copy-start | bytes 6148
  6.8 2.7 %collective-permute-start.1 = (s32[1,512]{1,0:T(1,128)}, s32[1,512]{1,0:T(1,128)S(1)}, u32[]{:S(2)}, u32[]{:S(2)}) collective-permute-start(s32[1,512]{1,0:T(1,128)} %bitcast.1), channel_id=1, source_target_pairs={{0,1},{1,0},{2,3},{3,2},{4,5},{5,4},{6,7},{7,6},{8,9},{9,8},{10,11... | collective-permute-start | bytes 6152 | tf_op jit(solution)/shard_map/ppermute | solution.py:269
  6.9 9.8 %collective-permute-start.5 = (s32[1,512]{1,0:T(1,128)}, s32[1,512]{1,0:T(1,128)S(1)}, u32[]{:S(2)}, u32[]{:S(2)}) collective-permute-start(s32[1,512]{1,0:T(1,128)} %bitcast.2), channel_id=1, source_target_pairs={{0,15},{1,0},{2,3},{3,5},{4,2},{5,4},{6,7},{7,9},{8,6},{9,8},{10,1... | collective-permute-start | bytes 6152 | tf_op jit(solution)/shard_map/ppermute | solution.py:269
  9.6 15.6 %collective-permute-start.3 = (s32[1,512]{1,0:T(1,128)S(1)}, s32[1,512]{1,0:T(1,128)S(1)}, u32[]{:S(2)}, u32[]{:S(2)}) collective-permute-start(s32[1,512]{1,0:T(1,128)S(1)} %bitcast.3), channel_id=1, source_target_pairs={{0,1},{1,3},{2,0},{3,2},{4,5},{5,7},{6,4},{7,6},{8,9},{9,11},{10,8... | collective-permute-start | bytes 6152 | tf_op jit(solution)/shard_map/ppermute | solution.py:269
  9.6 1.1 %copy-start = (bf16[512,768]{1,0:T(8,128)(2,1)S(1)}, bf16[512,768]{1,0:T(8,128)(2,1)}, u32[]{:S(2)}) copy-start(bf16[512,768]{1,0:T(8,128)(2,1)} %e_ref.1) | copy-start | bytes 2359300
  16.7 10.1 %collective-permute-start.6 = (f32[2,512]{1,0:T(2,128)S(1)}, f32[2,512]{1,0:T(2,128)S(1)}, u32[]{:S(2)}, u32[]{:S(2)}) collective-permute-start(f32[2,512]{1,0:T(2,128)S(1)} %get-tuple-element.22), channel_id=1, source_target_pairs={{15,0},{0,1},{3,2},{5,3},{2,4},{4,5},{7,6},{9,7},{6,8},{8,9},{11,1... | collective-permute-start | bytes 12296 | tf_op jit(solution)/shard_map/ppermute | solution.py:269
  26.0 1.4 %collective-permute-start.7 = (f32[2,512]{1,0:T(2,128)S(1)}, f32[2,512]{1,0:T(2,128)S(1)}, u32[]{:S(2)}, u32[]{:S(2)}) collective-permute-start(f32[2,512]{1,0:T(2,128)S(1)} %get-tuple-element.23), channel_id=1, source_target_pairs={{1,0},{3,1},{0,2},{2,3},{5,4},{7,5},{4,6},{6,7},{9,8},{11,9},{8,10... | collective-permute-start | bytes 12296 | tf_op jit(solution)/shard_map/ppermute | solution.py:269
  26.1 1.3 %collective-permute-start.8 = (f32[2,512]{1,0:T(2,128)S(1)}, f32[2,512]{1,0:T(2,128)S(1)}, u32[]{:S(2)}, u32[]{:S(2)}) collective-permute-start(f32[2,512]{1,0:T(2,128)S(1)} %shard_map.54), channel_id=1, source_target_pairs={{0,1},{1,0},{2,3},{3,2},{4,5},{5,4},{6,7},{7,6},{8,9},{9,8},{10,11... | collective-permute-start | bytes 12296 | tf_op jit(solution)/shard_map/ppermute | solution.py:269
